TPU v7x, 32 devices: a whole 2x2x4 slice. The times are simulated.
32 devices in a mesh: grp: 2 (over y), dev: 16 (over z, x, core).
Axes of the slice: x: 2, y: 2, z: 4, core: 2. Of those that a mesh axis runs over, the one named last changes fastest.
Arguments:
- series: float32 [2, 1024, 32768], P(None, None, ('grp', 'dev')), may hold values from -6 to 6
- templates: float32 [200, 128], replicated, may hold values from -0.5 to 0.5
- drift_template: int32 [16], replicated, may hold values from 0 to 199
- drift_reach: int32 [16], replicated, may hold values from 4 to 32, as said below
Outputs:
- powers: float32 [16, 33554432], P(None, ('grp', 'dev'))
Inputs may be any that keep to these rules, and one draw needn't show every extreme that they name: Drift d uses the taps t with 32 - drift_reach[d] <= t < 32 + drift_reach[d]; some drift uses all 64 taps.
All inputs are finite; a program needn't handle non-finite values.
Results may differ from a plain program's by a relative error of at most 0.000078.
Values sent between devices are 32-bit elements; how exact they have to be, the bound alone decides.
No kernel may reach another device: no remote copies, remote signals or barrier semaphores. Data moves between devices by JAX's collectives and lax.ppermute only.
A program may use at most 320 MiB of HBM per device.

v0:
```python
import math

import jax
import jax.numpy as jnp
from jax import lax
from jax.sharding import PartitionSpec as P

P1 = 32
P2 = 32
Q1 = 128
Q2 = 256
N = 67108864
M = 33554432
TAPS = 64


HIGHEST = lax.Precision.HIGHEST


def extended_2(block, sides, width):
    for axis, dim in sides:
        count = lax.axis_size(axis)
        forward = [(i, i + 1) for i in range(count - 1)]
        backward = [(target, source) for source, target in forward]
        low = lax.ppermute(
            lax.slice_in_dim(block, block.shape[dim] - width, None, axis=dim), axis, forward
        )
        high = lax.ppermute(lax.slice_in_dim(block, 0, width, axis=dim), axis, backward)
        block = jnp.concatenate([low, block, high], axis=dim)
    return block


def dft_table(length):
    indices = jnp.arange(length, dtype=jnp.int32)
    product = indices[:, None] * indices[None, :] % length
    angles = product.astype(jnp.float32) * (-2.0 * math.pi / length)
    return (jnp.cos(angles), jnp.sin(angles))


def twiddle(row_index, col_index, length):
    product = row_index[:, None] * col_index[None, :] % length
    angles = product.astype(jnp.float32) * (-2.0 * math.pi / length)
    return (jnp.cos(angles), jnp.sin(angles))


def complex_einsum(formula, left_pair, right_pair):
    left_real, left_imag = left_pair
    right_real, right_imag = right_pair
    real_part = jnp.einsum(formula, left_real, right_real, precision=HIGHEST) - jnp.einsum(
        formula, left_imag, right_imag, precision=HIGHEST
    )
    imag_part = jnp.einsum(formula, left_real, right_imag, precision=HIGHEST) + jnp.einsum(
        formula, left_imag, right_real, precision=HIGHEST
    )
    return (real_part, imag_part)


def complex_scale(values, factor):
    values_real, values_imag = values
    factor_real, factor_imag = factor
    return (
        values_real * factor_real - values_imag * factor_imag,
        values_real * factor_imag + values_imag * factor_real,
    )


def column_transform(series):
    col_count = series.shape[2]
    blocks = series.reshape(2, P1, P2, col_count)
    first_table = dft_table(P1)
    sectioned = (
        jnp.einsum("ja,eabc->ejbc", first_table[0], blocks, precision=HIGHEST),
        jnp.einsum("ja,eabc->ejbc", first_table[1], blocks, precision=HIGHEST),
    )
    inner_turn = twiddle(jnp.arange(P1, dtype=jnp.int32), jnp.arange(P2, dtype=jnp.int32), P1 * P2)
    sectioned = complex_scale(
        sectioned, (inner_turn[0][None, :, :, None], inner_turn[1][None, :, :, None])
    )
    sectioned = complex_einsum("kb,ejbc->ekjc", dft_table(P2), sectioned)
    return (
        sectioned[0].reshape(2, P1 * P2, col_count),
        sectioned[1].reshape(2, P1 * P2, col_count),
    )


def row_transform(values):
    parts_count, row_count = (values[0].shape[0], values[0].shape[1])
    shaped = (
        values[0].reshape(parts_count, row_count, Q1, Q2),
        values[1].reshape(parts_count, row_count, Q1, Q2),
    )
    sectioned = complex_einsum("ja,kbac->kbjc", dft_table(Q1), shaped)
    inner_turn = twiddle(jnp.arange(Q1, dtype=jnp.int32), jnp.arange(Q2, dtype=jnp.int32), Q1 * Q2)
    sectioned = complex_scale(sectioned, (inner_turn[0][None, None], inner_turn[1][None, None]))
    sectioned = complex_einsum("lc,kbjc->kblj", dft_table(Q2), sectioned)
    return (
        sectioned[0].reshape(parts_count, row_count, Q1 * Q2),
        sectioned[1].reshape(parts_count, row_count, Q1 * Q2),
    )


def combine_halves(even_part, odd_part, frequency):
    angles = frequency.astype(jnp.float32) * (-2.0 * math.pi / N)
    turned = complex_scale(odd_part, (jnp.cos(angles), jnp.sin(angles)))
    norm_scale = 1.0 / math.sqrt(N)
    return ((even_part[0] + turned[0]) * norm_scale, (even_part[1] + turned[1]) * norm_scale)


def to_rows(stacked):
    group_count = lax.axis_size("grp")
    member_count = lax.axis_size("dev")
    leading = stacked.shape[0]
    col_count = stacked.shape[2]
    row_count = stacked.shape[1] // (group_count * member_count)
    shaped = stacked.reshape(leading, group_count, member_count, row_count, 1, 1, col_count)
    arrived = lax.all_to_all(
        lax.all_to_all(shaped, "grp", split_axis=1, concat_axis=4, tiled=True),
        "dev",
        split_axis=2,
        concat_axis=5,
        tiled=True,
    )
    return arrived.reshape(leading, row_count, group_count * member_count * col_count)


def to_segments(stacked):
    group_count = lax.axis_size("grp")
    member_count = lax.axis_size("dev")
    leading = stacked.shape[0]
    row_count = stacked.shape[1]
    col_count = stacked.shape[2] // (group_count * member_count)
    shaped = stacked.reshape(leading, 1, 1, row_count, group_count, member_count, col_count)
    arrived = lax.all_to_all(
        lax.all_to_all(shaped, "grp", split_axis=4, concat_axis=1, tiled=True),
        "dev",
        split_axis=5,
        concat_axis=2,
        tiled=True,
    )
    gathered = arrived.reshape(leading, group_count * member_count * row_count, col_count)
    return jnp.swapaxes(gathered, 1, 2).reshape(
        leading, col_count * group_count * member_count * row_count
    )


def tap_kernels(templates, drift_template, drift_reach):
    template_count = templates.shape[0]
    selector = (
        drift_template[:, None] == jnp.arange(template_count, dtype=jnp.int32)[None, :]
    ).astype(jnp.float32)
    chosen = jnp.dot(selector, templates, precision=HIGHEST, preferred_element_type=jnp.float32)
    taps_index = jnp.arange(TAPS, dtype=jnp.int32)[None, :]
    center = TAPS // 2
    inside = (
        (taps_index >= center - drift_reach[:, None]) & (taps_index < center + drift_reach[:, None])
    ).astype(jnp.float32)
    return (chosen[:, :TAPS] * inside, chosen[:, TAPS:] * inside)


def banded(kernel_rows, window_width):
    lane_width = 128
    drift_count = kernel_rows.shape[0]
    padded = jnp.concatenate(
        [kernel_rows, jnp.zeros((drift_count, window_width + 1 - TAPS), jnp.float32)], axis=1
    )
    tiled_rows = jnp.tile(padded, (1, lane_width))[:, : lane_width * window_width]
    return jnp.swapaxes(tiled_rows.reshape(drift_count, lane_width, window_width), 1, 2)


def correlate(extended, kernels, segment_bins):
    lane_width = 128
    row_count = segment_bins // lane_width
    window_width = lane_width + TAPS
    head_rows = extended[:, :segment_bins].reshape(2, row_count, lane_width)
    rest_bins = jnp.concatenate(
        [extended[:, lane_width:], jnp.zeros((2, lane_width - TAPS), jnp.float32)], axis=1
    )
    tail_rows = rest_bins.reshape(2, row_count, lane_width)[:, :, :TAPS]
    windows = jnp.concatenate([head_rows, tail_rows], axis=2)
    flat_windows = jnp.concatenate([windows[0], windows[1]], axis=1)
    band_real = banded(kernels[0], window_width)
    band_imag = banded(kernels[1], window_width)
    matrices = jnp.concatenate(
        [
            jnp.concatenate([band_real, band_imag], axis=2),
            jnp.concatenate([-band_imag, band_real], axis=2),
        ],
        axis=1,
    )
    response = jnp.einsum(
        "rw,dwo->dro", flat_windows, matrices, precision=HIGHEST, preferred_element_type=jnp.float32
    )
    power_rows = (
        response[:, :, :lane_width] * response[:, :, :lane_width]
        + response[:, :, lane_width:] * response[:, :, lane_width:]
    )
    return power_rows.reshape(power_rows.shape[0], row_count * lane_width)


def local(series, templates, drift_template, drift_reach):
    position = lax.axis_index(("grp", "dev"))
    col_count = series.shape[2]
    row_total = P1 * P2
    row_frequency = jnp.arange(row_total, dtype=jnp.int32)
    columns = position * col_count + jnp.arange(col_count, dtype=jnp.int32)
    column_turn = twiddle(row_frequency, columns, M)
    section_real, section_imag = column_transform(series)
    turned = complex_scale(
        (section_real, section_imag), (column_turn[0][None], column_turn[1][None])
    )
    by_rows = to_rows(jnp.concatenate([turned[0], turned[1]], axis=0))
    spectrum = row_transform((by_rows[0:2], by_rows[2:4]))
    row_count = by_rows.shape[1]
    row_index = position * row_count + jnp.arange(row_count, dtype=jnp.int32)
    frequency = row_index[:, None] + row_total * jnp.arange(Q1 * Q2, dtype=jnp.int32)[None, :]
    whole_real, whole_imag = combine_halves(
        (spectrum[0][0], spectrum[1][0]), (spectrum[0][1], spectrum[1][1]), frequency
    )
    segment = to_segments(jnp.stack([whole_real, whole_imag]))
    segment_bins = segment.shape[1]
    kernels = tap_kernels(templates, drift_template, drift_reach)
    extended = extended_2(segment, ((("grp", "dev"), 1),), TAPS // 2)
    return correlate(extended, kernels, segment_bins)


def solution(mesh):
    return jax.shard_map(
        local,
        mesh=mesh,
        in_specs=(P(None, None, ("grp", "dev")), P(), P(), P()),
        out_specs=P(None, ("grp", "dev")),
        check_vma=False,
    )
```

profile of v0, /device:TPU:4, one launch (start us, length us, event | category | flops | bytes accessed | tf_op | source)
XLA Modules:
  0.0 1793.5 jit_solution(16533184697861309207)
XLA Ops:
  0.3 17.4 fusion.18
  17.7 17.1 subtract_bitcast_fusion.1
  34.9 14.2 fusion.10
  49.1 14.5 fusion.12
  63.5 20.6 %fusion.34 = f32[2,32,1024,32]{2,3,1,0:T(8,128)S(1)} fusion(f32[2,32,1024,32]{2,3,1,0:T(8,128)} %fusion.12, f32[2,32,32,1024]{3,1,2,0:T(8,128)} %get-tuple-element.9), kind=kOutput, calls=%fused_computation.66 | convolution fusion | flops 807417856 | bytes 25165824 | tf_op jit(solution)/shard_map/kb,ejbc->ekjc/dot_general | solution.py:49
  84.2 19.7 %fusion.37 = f32[2,32,1024,32]{2,3,1,0:T(8,128)} fusion(f32[2,32,1024,32]{2,3,1,0:T(8,128)S(1)} %copy-done.5, f32[2,32,32,1024]{3,1,2,0:T(8,128)} %get-tuple-element.9), kind=kOutput, calls=%fused_computation.67 | convolution fusion | flops 807417856 | bytes 25165824 | tf_op jit(solution)/shard_map/kb,ejbc->ekjc/dot_general | solution.py:52
  103.9 18.9 %fusion.41 = (f32[2,16,32,1024]{3,1,2,0:T(8,128)}, f32[2,16,32,1024]{3,1,2,0:T(8,128)}) fusion(s32[1024]{0:T(1024)S(1)} %iota_add_fusion, s32[2,16,32]{1,2,0:T(8,128)S(1)} %multiply_add_fusion.1), kind=kLoop, calls=%fused_computation.69 | loop fusion | flops 14680064 | bytes 8396800 | tf_op jit(solution)/shard_map/cos | solution.py:43
  122.8 11.4 multiply_subtract_fusion
  134.1 7.0 pad_maximum_fusion
  141.1 184.2 %all_to_all.66 = f32[4,2,16,32,1,1,1024]{6,2,3,0,5,4,1:T(8,128)S(1)} all-to-all(f32[4,2,16,32,1,1,1024]{6,2,3,0,5,4,1:T(8,128)S(1)} %pad_maximum_fusion), channel_id=1, replica_groups=mesh['grp'=2,'dev'=16] {'grp'}, dimensions={1} | all-to-all | bytes 33554432 | tf_op jit(solution)/shard_map/all_to_all | solution.py:117
  325.3 17.9 copy.74
  343.2 7.0 all-to-all-start.1
  350.8 296.0 %all-to-all-done.1 = f32[4,1,16,32,2,1,1024]{6,4,3,0,5,1,2:T(2,128)} async-done(((f32[4,1,16,32,2,1,1024]{6,4,3,0,5,1,2:T(2,128)}), f32[4,1,16,32,2,1,1024]{6,4,3,0,5,1,2:T(2,128)}, u32[]{:S(2)}, u32[]{:S(2)}) %all-to-all-start.1) | async-done | bytes 16777248 | tf_op jit(solution)/shard_map/all_to_all | solution.py:116
  646.8 13.1 fusion.175
  659.9 8.1 copy.75
  668.0 9.8 reshape.404
  677.8 17.3 fusion.69
  695.2 16.3 fusion.75
  711.5 8.3 copy.77
  719.7 9.9 reshape.405
  729.7 17.2 fusion.71
  746.8 24.6 %fusion.8 = (f32[2,32,128,256]{2,3,1,0:T(8,128)}, f32[2,32,128,256]{2,3,1,0:T(8,128)}) fusion(f32[128,256]{0,1:T(8,128)S(1)} %get-tuple-element.31, f32[128,256]{0,1:T(8,128)S(1)} %get-tuple-element.32, f32[2,32,256,128]{3,2,1,0:T(8,128)} %fusion.69, f32[2,32,256,128]{3,2,1,0:T(8,128)} %fusion.75, f32[2,32,256,128]{3,2,1,0:T(8,128)} %fusion.71, ...), kind=kOutput, calls=%fused_computation.24 | convolution fusion | flops 3238232064 | bytes 50593792 | tf_op jit(solution)/shard_map/ja,kbac->kbjc/dot_general | solution.py:52
  771.4 19.9 %fusion.49 = f32[2,32,128,256]{3,2,1,0:T(8,128)} fusion(f32[2,32,128,256]{2,3,1,0:T(8,128)} %get-tuple-element.5), kind=kOutput, calls=%fused_computation.80 | convolution fusion | flops 6443368448 | bytes 16777216 | tf_op jit(solution)/shard_map/lc,kbjc->kblj/dot_general | solution.py:49
  791.3 15.1 fusion.47
  806.5 20.6 %subtract_bitcast_fusion = f32[2,32,256,128]{2,3,1,0:T(8,128)} fusion(f32[2,32,128,256]{3,2,1,0:T(8,128)} %fusion.49, f32[2,32,128,256]{2,3,1,0:T(8,128)S(1)} %copy-done.3), kind=kOutput, calls=%fused_computation.29 | convolution fusion | flops 6445465600 | bytes 25165824 | tf_op jit(solution)/shard_map/lc,kbjc->kblj/dot_general | solution.py:49
  827.1 18.8 %add_bitcast_fusion = f32[2,32,256,128]{2,3,1,0:T(8,128)} fusion(f32[2,32,128,256]{3,2,1,0:T(8,128)S(1)} %fusion.47, f32[2,32,128,256]{2,3,1,0:T(8,128)S(1)} %bitcast.159), kind=kOutput, calls=%fused_computation.28 | convolution fusion | flops 6445465600 | bytes 25165824 | tf_op jit(solution)/shard_map/lc,kbjc->kblj/dot_general | solution.py:52
  845.9 7.7 fusion.178
  853.6 5.6 copy.87
  859.2 4.9 squeeze.20
  864.1 7.8 fusion.177
  871.9 5.6 copy.83
  877.5 4.9 squeeze.18
  882.4 5.6 copy.84
  888.0 4.9 squeeze.19
  892.9 5.6 copy.88
  898.5 5.0 squeeze.21
  903.4 19.2 %add_multiply_fusion.1 = (f32[1,1,1,32,2,16,1024]{6,5,4,3,2,1,0:T(8,128)S(1)}, f32[1,1,1,32,2,16,1024]{6,5,4,3,2,1,0:T(8,128)S(1)}) fusion(f32[1,1,1,32,2,16,1024]{6,5,4,3,2,1,0:T(8,128)} %squeeze.18, f32[1,1,1,32,2,16,1024]{6,5,4,3,2,1,0:T(8,128)} %squeeze.20, f32[1,1,1,32,2,16,1024]{6,5,4,3,2,1,0:T(8,128)} %squeeze.19, ...), kind=kLoop, calls=%fused_computation.62 | loop fusion | flops 13631488 | bytes 25297024 | tf_op jit(solution)/shard_map/mul | solution.py:106
  922.6 1.7 pad_maximum_fusion.3
  924.3 1.7 copy.89
  926.0 96.2 %all_to_all.67 = f32[2,1,1,32,2,16,1024]{6,5,3,2,1,0,4:T(8,128)S(1)} all-to-all(f32[2,1,1,32,2,16,1024]{6,5,3,2,1,0,4:T(8,128)S(1)} %copy.89), channel_id=1, replica_groups=mesh['grp'=2,'dev'=16] {'grp'}, dimensions={4} | all-to-all | bytes 16777216 | tf_op jit(solution)/shard_map/all_to_all | solution.py:134
  1022.2 9.1 copy.90
  1031.3 70.4 %all-to-all-start.3 = ((f32[2,2,1,32,1,16,1024]{6,1,3,0,4,2,5:T(2,128)}), f32[2,2,1,32,1,16,1024]{6,1,3,0,4,2,5:T(2,128)}, u32[]{:S(2)}, u32[]{:S(2)}) async-start(f32[2,2,1,32,1,16,1024]{6,1,3,0,4,2,5:T(2,128)} %copy.90), calls=%async_computation.3 | async-start | bytes 16777216 | tf_op jit(solution)/shard_map/all_to_all | solution.py:133
  1102.2 2.2 tile.21
  1104.4 2.7 slice.89
  1107.0 2.3 reshape.400
  1109.4 1.6 bitcast_negate_fusion
  1111.0 141.3 %all-to-all-done.3 = f32[2,2,1,32,1,16,1024]{6,1,3,0,4,2,5:T(2,128)} async-done(((f32[2,2,1,32,1,16,1024]{6,1,3,0,4,2,5:T(2,128)}), f32[2,2,1,32,1,16,1024]{6,1,3,0,4,2,5:T(2,128)}, u32[]{:S(2)}, u32[]{:S(2)}) %all-to-all-start.3) | async-done | bytes 8388640 | tf_op jit(solution)/shard_map/all_to_all | solution.py:133
  1252.2 9.3 copy.91
  1261.5 8.8 copy.92
  1270.3 14.4 copy.108
  1284.7 3.4 copy-done.4
  1288.2 2.9 collective-permute-start
  1291.0 37.4 %collective-permute-start.1 = (f32[2,32]{1,0:T(2,128)S(1)}, f32[2,32]{1,0:T(2,128)S(1)}, u32[]{:S(2)}, u32[]{:S(2)}) collective-permute-start(f32[2,32]{1,0:T(2,128)S(1)} %get-tuple-element.20), channel_id=1, source_target_pairs={{1,0},{2,1},{3,2},{4,3},{5,4},{6,5},{7,6},{8,7},{9,8},{10,9},{11,1... | collective-permute-start | bytes 776 | tf_op jit(solution)/shard_map/ppermute | solution.py:28
  1330.0 3.8 tile.9
  1333.7 2.7 slice.87
  1336.4 3.7 reshape.399
  1340.2 28.8 %fusion.7 = (f32[1,2,8192,128]{3,1,2,0:T(2,128)S(1)}, f32[1,2,8192,128]{3,1,2,0:T(2,128)S(1)}) fusion(f32[2,1048576]{1,0:T(2,128)} %bitcast.162, f32[2,32]{1,0:T(2,128)S(1)} %collective-permute-done, f32[2,32]{1,0:T(2,128)S(1)} %collective-permute-done.1), kind=kLoop, calls=%fused_computation.20 | loop fusion | flops 10485760 | bytes 25166336
  1368.9 3.9 copy.139
  1372.9 3.8 copy.138
  1376.7 10.0 fusion.4
  1386.7 223.8 %convolution_bitcast_fusion = f32[16,8192,256]{1,2,0:T(8,128)} fusion(f32[8192,192]{1,0:T(8,128)} %get-tuple-element.12, f32[8192,192]{1,0:T(8,128)S(1)} %get-tuple-element.11, f32[16,192,128]{1,2,0:T(8,128)} %bitcast.175, f32[16,192,128]{1,2,0:T(8,128)} %bitcast_negate_fusion, f32[16,192,128]{1,2,0:T(8,128)S(1)} %bitcast.174), kind=kOutput, calls=%fused_computation | convolution fusion | flops 154626686976 | bytes 151519232 | tf_op jit(solution)/shard_map/rw,dwo->dro/dot_general | solution.py:190
  1610.5 64.7 %fusion = f32[16,8192,128]{1,2,0:T(8,128)} fusion(f32[16,8192,256]{1,2,0:T(8,128)} %convolution_bitcast_fusion), kind=kLoop, calls=%fused_computation.3 | loop fusion | flops 50331648 | bytes 201326592 | tf_op jit(solution)/shard_map/add | solution.py:194
  1675.3 61.1 %copy.93 = f32[16,8192,128]{2,1,0:T(8,128)} copy(f32[16,8192,128]{1,2,0:T(8,128)} %fusion) | data formatting | bytes 134217728 | tf_op jit(solution)/shard_map/add | solution.py:194
  1736.4 56.6 %copy.137 = f32[2,8,8192,128]{3,1,2,0:T(8,128)} copy(f32[2,8,8192,128]{3,2,1,0:T(8,128)} %bitcast.71) | data formatting | bytes 134217728
  (46 shorter events, 3.0 us)
Async XLA Ops:
  0.0 1101.7 %copy-start = (f32[200,128]{1,0:T(8,128)S(1)}, f32[200,128]{1,0:T(8,128)}, u32[]{:S(2)}) copy-start(f32[200,128]{1,0:T(8,128)} %param.5) | copy-start | bytes 307204
  0.3 17.4 copy-start.6
  63.5 20.7 %copy-start.5 = (f32[2,32,1024,32]{2,3,1,0:T(8,128)S(1)}, f32[2,32,1024,32]{2,3,1,0:T(8,128)}, u32[]{:S(2)}) copy-start(f32[2,32,1024,32]{2,3,1,0:T(8,128)} %fusion.10) | copy-start | bytes 25165828
  343.2 303.6 %all-to-all-start.1 = ((f32[4,1,16,32,2,1,1024]{6,4,3,0,5,1,2:T(2,128)}), f32[4,1,16,32,2,1,1024]{6,4,3,0,5,1,2:T(2,128)}, u32[]{:S(2)}, u32[]{:S(2)}) async-start(f32[4,1,16,32,2,1,1024]{6,4,3,0,5,1,2:T(2,128)} %copy.74), calls=%async_computation.1 | async-start | bytes 33554432 | tf_op jit(solution)/shard_map/all_to_all | solution.py:116
  677.8 17.3 copy-start.2
  677.8 33.6 %slice-start.2 = ((s8[8388608]{0:T(1024)(128)(4,1)}), s8[4194304]{0:T(1024)(128)(4,1)S(1)}, s32[]{:S(2)}) async-start(s8[8388608]{0:T(1024)(128)(4,1)} %bitcast.170), calls=%async_computation.6 | async-start | bytes 8388608
  695.2 16.3 slice-start.3
  771.4 19.9 %copy-start.3 = (f32[2,32,128,256]{2,3,1,0:T(8,128)S(1)}, f32[2,32,128,256]{2,3,1,0:T(8,128)}, u32[]{:S(2)}) copy-start(f32[2,32,128,256]{2,3,1,0:T(8,128)} %get-tuple-element.6) | copy-start | bytes 25165828
  791.3 35.8 %slice-start = ((s8[8388608]{0:T(1024)(128)(4,1)}), s8[4194304]{0:T(1024)(128)(4,1)S(1)}, s32[]{:S(2)}) async-start(s8[8388608]{0:T(1024)(128)(4,1)} %bitcast.158), calls=%async_computation.4 | async-start | bytes 8388608
  806.5 20.6 %slice-start.1 = ((s8[8388608]{0:T(1024)(128)(4,1)}), s8[4194304]{0:T(1024)(128)(4,1)S(1)}, s32[]{:S(2)}) async-start(s8[8388608]{0:T(1024)(128)(4,1)} %bitcast.158), calls=%async_computation.5 | async-start | bytes 8388608
  1031.3 70.4 %copy-start.8 = (s32[16]{0:T(128)S(1)}, s32[16]{0:T(128)}, u32[]{:S(2)}) copy-start(s32[16]{0:T(128)} %param.7) | copy-start | bytes 196
  1031.3 70.4 %copy-start.7 = (s32[16]{0:T(128)S(1)}, s32[16]{0:T(128)}, u32[]{:S(2)}) copy-start(s32[16]{0:T(128)} %param.6) | copy-start | bytes 196
  1031.3 220.9 %all-to-all-start.3 = ((f32[2,2,1,32,1,16,1024]{6,1,3,0,4,2,5:T(2,128)}), f32[2,2,1,32,1,16,1024]{6,1,3,0,4,2,5:T(2,128)}, u32[]{:S(2)}, u32[]{:S(2)}) async-start(f32[2,2,1,32,1,16,1024]{6,1,3,0,4,2,5:T(2,128)} %copy.90), calls=%async_computation.3 | async-start | bytes 16777216 | tf_op jit(solution)/shard_map/all_to_all | solution.py:133
  1284.7 3.4 copy-start.4
  1288.2 52.0 %collective-permute-start = (f32[2,32]{1,0:T(2,128)S(1)}, f32[2,32]{1,0:T(2,128)S(1)}, u32[]{:S(2)}, u32[]{:S(2)}) collective-permute-start(f32[2,32]{1,0:T(2,128)S(1)} %get-tuple-element.19), channel_id=1, source_target_pairs={{0,1},{1,2},{2,3},{3,4},{4,5},{5,6},{6,7},{7,8},{8,9},{9,10},{10,1... | collective-permute-start | bytes 776 | tf_op jit(solution)/shard_map/ppermute | solution.py:25
  1291.0 49.1 %collective-permute-start.1 = (f32[2,32]{1,0:T(2,128)S(1)}, f32[2,32]{1,0:T(2,128)S(1)}, u32[]{:S(2)}, u32[]{:S(2)}) collective-permute-start(f32[2,32]{1,0:T(2,128)S(1)} %get-tuple-element.20), channel_id=1, source_target_pairs={{1,0},{2,1},{3,2},{4,3},{5,4},{6,5},{7,6},{8,7},{9,8},{10,9},{11,1... | collective-permute-start | bytes 776 | tf_op jit(solution)/shard_map/ppermute | solution.py:28
  1736.4 56.6 %copy-start.1 = (f32[200,128]{1,0:T(8,128)S(1)}, f32[200,128]{1,0:T(8,128)}, u32[]{:S(2)}) copy-start(f32[200,128]{1,0:T(8,128)} %param.5) | copy-start | bytes 307204
where the time goes:
time: 1800 us; the launch traced here: 1790 us
  matrix products  477 us (26%)
  waiting for transfers between devices  437 us (24%)
  local copies, waits for them, and re-layouts  316 us (18%)
  blocking collectives  280 us (16%)
  other arithmetic  164 us (9%)
  starting transfers between devices  118 us (7%)
    all_to_all x1, waiting for transfers between devices, to_rows(): lax.all_to_all(lax.all_to_all(shaped, 'grp', split_axis=1, concat_axis=4,...  296 us
    dot_general x1, matrix products, correlate(): jnp.einsum('rw,dwo->dro', flat_windows, matrices, precision=HIGHEST, pref...  224 us
    all_to_all x1, blocking collectives, to_rows(): lax.all_to_all(shaped, 'grp', split_axis=1, concat_axis=4, tiled=True)  184 us
    all_to_all x1, waiting for transfers between devices, to_segments(): lax.all_to_all(lax.all_to_all(shaped, 'grp', split_axis=4, concat_axis=1,...  141 us
    all_to_all x1, blocking collectives, to_segments(): lax.all_to_all(shaped, 'grp', split_axis=4, concat_axis=1, tiled=True)  96.2 us
    unnamed x30, local copies, waits for them, and re-layouts  82.2 us
    all_to_all x1, starting transfers between devices, to_segments(): lax.all_to_all(lax.all_to_all(shaped, 'grp', split_axis=4, concat_axis=1,...  70.4 us
    add x1, other arithmetic, correlate(): response[:, :, :lane_width] * response[:, :, :lane_width]  64.7 us
  transfers between devices with their start and end apart: 4, of which 2 were waited for; matrix products, arithmetic and copies ran while one was open for 1% of the time, Pallas kernels for 0%

commit v1 on v0

--- a/solution.py
+++ b/solution.py
@@ -1,9 +1,39 @@
+import functools
 import math
 
 import jax
 import jax.numpy as jnp
 from jax import lax
+from jax.experimental import pallas as pl
+from jax.experimental.pallas import tpu as pltpu
 from jax.sharding import PartitionSpec as P
+
+AXES = ("grp", "dev")
+LANES = 128
+SUBLANES = 8
+VMEM_LIMIT = 60 * 1024 * 1024
+F32 = jnp.float32
+BF16 = jnp.bfloat16
+
+
+def split(x):
+    high = x.astype(BF16)
+    return high, (x - high.astype(F32)).astype(BF16)
+
+
+def split_xla(x):
+    high = lax.reduce_precision(x, 8, 7)
+    return high.astype(BF16), lax.reduce_precision(x - high, 8, 7).astype(BF16)
+
+
+def phases(product, length):
+    angles = (product % length).astype(F32) * (2.0 * math.pi / length)
+    return jnp.cos(angles), jnp.sin(angles)
+
+
+def iota(count):
+    return jnp.arange(count, dtype=jnp.int32)
+
 
 P1 = 32
 P2 = 32
@@ -12,8 +42,6 @@
 N = 67108864
 M = 33554432
 TAPS = 64
-
-
 HIGHEST = lax.Precision.HIGHEST
 
 
@@ -143,7 +171,7 @@
     )
 
 
-def tap_kernels(templates, drift_template, drift_reach):
+def general_taps(templates, drift_template, drift_reach):
     template_count = templates.shape[0]
     selector = (
         drift_template[:, None] == jnp.arange(template_count, dtype=jnp.int32)[None, :]
@@ -157,7 +185,7 @@
     return (chosen[:, :TAPS] * inside, chosen[:, TAPS:] * inside)
 
 
-def banded(kernel_rows, window_width):
+def general_banded(kernel_rows, window_width):
     lane_width = 128
     drift_count = kernel_rows.shape[0]
     padded = jnp.concatenate(
@@ -178,8 +206,8 @@
     tail_rows = rest_bins.reshape(2, row_count, lane_width)[:, :, :TAPS]
     windows = jnp.concatenate([head_rows, tail_rows], axis=2)
     flat_windows = jnp.concatenate([windows[0], windows[1]], axis=1)
-    band_real = banded(kernels[0], window_width)
-    band_imag = banded(kernels[1], window_width)
+    band_real = general_banded(kernels[0], window_width)
+    band_imag = general_banded(kernels[1], window_width)
     matrices = jnp.concatenate(
         [
             jnp.concatenate([band_real, band_imag], axis=2),
@@ -197,7 +225,7 @@
     return power_rows.reshape(power_rows.shape[0], row_count * lane_width)
 
 
-def local(series, templates, drift_template, drift_reach):
+def general_local(series, templates, drift_template, drift_reach):
     position = lax.axis_index(("grp", "dev"))
     col_count = series.shape[2]
     row_total = P1 * P2
@@ -218,16 +246,403 @@
     )
     segment = to_segments(jnp.stack([whole_real, whole_imag]))
     segment_bins = segment.shape[1]
-    kernels = tap_kernels(templates, drift_template, drift_reach)
+    kernels = general_taps(templates, drift_template, drift_reach)
     extended = extended_2(segment, ((("grp", "dev"), 1),), TAPS // 2)
     return correlate(extended, kernels, segment_bins)
+
+
+def column_kernel(x_ref, table_ref, base_re_ref, base_im_ref, step_re_ref, step_im_ref, o_ref):
+    slots = base_re_ref.shape[0]
+    rows = x_ref.shape[1]
+    width = x_ref.shape[2]
+    block = pl.program_id(0)
+    blocks = pl.num_programs(0)
+    x = jnp.concatenate([x_ref[0], x_ref[1]], axis=1)
+    high, low = split(x)
+    out = jnp.dot(
+        table_ref[...], jnp.concatenate([high, high], axis=0), preferred_element_type=F32
+    ) + jnp.dot(table_ref[:, :rows], low, preferred_element_type=F32)
+    base_re = base_re_ref[...]
+    base_im = base_im_ref[...]
+    for chunk in range(2 * width // LANES):
+        lanes = slice(chunk * LANES, (chunk + 1) * LANES)
+        step_re = step_re_ref[0, :, chunk : chunk + 1]
+        step_im = step_im_ref[0, :, chunk : chunk + 1]
+        turn_re = base_re * step_re - base_im * step_im
+        turn_im = base_re * step_im + base_im * step_re
+        real = out[:slots, lanes]
+        imag = out[slots:, lanes]
+        pitch = 2 * width // LANES * SUBLANES
+        start = chunk * SUBLANES + block
+        o_ref[pl.ds(start, slots, stride=pitch), :] = real * turn_re + imag * turn_im
+        o_ref[pl.ds(start + blocks, slots, stride=pitch), :] = imag * turn_re - real * turn_im
+
+
+def column_stage(series, position, width):
+    rows, cols = series.shape[1], series.shape[2]
+    slots = rows // 2
+    blocks = cols // width
+    samples = 2 * rows * cols * lax.axis_size(AXES)
+    slot = iota(slots)
+    near_re, near_im = phases(slot[:, None] * iota(LANES)[None, :], rows)
+    far_re, far_im = phases(slot[:, None] * (LANES * iota(rows // LANES))[None, :], rows)
+    cos = jnp.concatenate(
+        [near_re * far_re[:, i : i + 1] - near_im * far_im[:, i : i + 1] for i in range(rows // LANES)],
+        axis=1,
+    )
+    sin = jnp.concatenate(
+        [near_re * far_im[:, i : i + 1] + near_im * far_re[:, i : i + 1] for i in range(rows // LANES)],
+        axis=1,
+    )
+    alternating = (1 - 2 * (iota(rows) % 2)).astype(F32)[None, :]
+    sin = jnp.where(slot[:, None] == 0, alternating, -sin)
+    table = jnp.concatenate(split_xla(jnp.concatenate([cos, sin], axis=0)), axis=1)
+    base_re, base_im = phases(slot[:, None] * (2 * iota(LANES))[None, :], samples)
+    chunks = width // LANES
+    start = (
+        2 * (position * cols + width * iota(blocks)[:, None, None] + LANES * iota(chunks)[None, None, :])
+        + iota(2)[None, :, None]
+    ).reshape(blocks, 1, 2 * chunks)
+    step_re, step_im = phases(start * slot[None, :, None], samples)
+    small = pl.BlockSpec((1, slots, 2 * chunks), lambda i: (i, 0, 0))
+    whole = lambda a: pl.BlockSpec(a.shape, lambda i: (0, 0))
+    return pl.pallas_call(
+        column_kernel,
+        grid=(blocks,),
+        in_specs=[
+            pl.BlockSpec((2, rows, width), lambda i: (0, 0, i)),
+            whole(table),
+            whole(base_re),
+            whole(base_im),
+            small,
+            small,
+        ],
+        out_specs=pl.BlockSpec((slots * 2 * chunks * SUBLANES, LANES), lambda i: (0, 0)),
+        out_shape=jax.ShapeDtypeStruct((slots * 2 * chunks * SUBLANES, LANES), F32),
+        compiler_params=pltpu.CompilerParams(vmem_limit_bytes=VMEM_LIMIT),
+        name="columns",
+    )(series, table, base_re, base_im, step_re, step_im)
+
+
+def row_kernel(variant_ref, x_ref, first_ref, turn_ref, second_ref, o_ref):
+    depth = first_ref.shape[2] // 3
+    count, width = turn_ref.shape[3], turn_ref.shape[4]
+    x = [x_ref[:, 0, i].reshape(depth, LANES) for i in range(width // LANES)]
+    high, low = split(jnp.concatenate(x, axis=1))
+    out = jnp.dot(
+        first_ref[0], jnp.concatenate([high, high, low], axis=0), preferred_element_type=F32
+    )
+    pieces = []
+    for side in range(2):
+        real = out[2 * side * count : (2 * side + 1) * count]
+        imag = out[(2 * side + 1) * count : (2 * side + 2) * count]
+        turn_re = turn_ref[0, side, 0]
+        turn_im = turn_ref[0, side, 1]
+        turned = jnp.concatenate(
+            [real * turn_re + imag * turn_im, imag * turn_re - real * turn_im], axis=1
+        )
+        high, low = split(turned)
+        pieces.append(jnp.concatenate([high, high, low], axis=1))
+    result = lax.dot_general(
+        second_ref[...],
+        jnp.concatenate(pieces, axis=0),
+        (((1,), (1,)), ((), ())),
+        preferred_element_type=F32,
+    )
+    half = result.shape[0] // 2
+    for side in range(2):
+        for part in range(2):
+            block = result[part * half : (part + 1) * half, side * count : (side + 1) * count]
+            o_ref[:, side, part, 0] = block.reshape(half // SUBLANES, SUBLANES, count)
+
+
+def row_stage(arrived, position, total_rows, samples):
+    devices, slots, chunks, sublanes, _ = arrived.shape
+    width = chunks * LANES
+    inner = sublanes // 2
+    count = devices * inner
+    lines = width // 2
+    freq = iota(count)[:, None]
+    order = (inner * iota(devices)[:, None] + iota(inner)[None, :]).reshape(1, devices, inner)
+    fc, fs = phases(freq[:, :, None] * order, count)
+    bc, bs = phases((freq[:, :, None] + 1) * order, count)
+    hc, hs = phases((2 * freq[:, :, None] + 1) * order, 2 * count)
+    zero = jnp.zeros_like(fc)
+    pack = lambda on_re, on_im: jnp.stack([on_re, on_im], axis=2).reshape(count, devices * sublanes)
+    usual = jnp.concatenate([pack(fc, fs), pack(-fs, fc), pack(bc, -bs), pack(-bs, -bc)], axis=0)
+    special = jnp.concatenate(
+        [pack(fc, zero), pack(-fs, zero), pack(zero, hc), pack(zero, -hs)], axis=0
+    )
+    high, low = split_xla(jnp.stack([usual, special]))
+    first = jnp.concatenate([high, low, high], axis=2)
+    beta = (2 * iota(lines)[None, :] + iota(2)[:, None]).reshape(1, width)
+    length = count * width
+    turn_a = jnp.stack(phases(freq * beta, length))
+    turn_b = jnp.stack(phases((freq + 1) * beta, length))
+    turn_c = jnp.stack(phases((2 * freq + 1) * beta, 2 * length))
+    turn = jnp.stack([jnp.stack([turn_a, turn_b]), jnp.stack([turn_a, turn_c])])
+    gc, gs = phases(iota(lines)[:, None] * beta, width)
+    second = jnp.concatenate(
+        [jnp.concatenate([gc, gs], axis=1), jnp.concatenate([-gs, gc], axis=1)], axis=0
+    ) * (1.0 / math.sqrt(samples))
+    high, low = split_xla(second)
+    second = jnp.concatenate([high, low, high], axis=1)
+    variant = jnp.where((iota(slots) == 0) & (position == 0), 1, 0).astype(jnp.int32)
+    blocks = lines // SUBLANES
+    shape = (blocks, 2, 2, slots, SUBLANES, count)
+    return pl.pallas_call(
+        row_kernel,
+        grid_spec=pltpu.PrefetchScalarGridSpec(
+            num_scalar_prefetch=1,
+            grid=(slots,),
+            in_specs=[
+                pl.BlockSpec((devices, 1, chunks, sublanes, LANES), lambda i, v: (0, i, 0, 0, 0)),
+                pl.BlockSpec((1,) + first.shape[1:], lambda i, v: (v[i], 0, 0)),
+                pl.BlockSpec((1,) + turn.shape[1:], lambda i, v: (v[i], 0, 0, 0, 0)),
+                pl.BlockSpec(second.shape, lambda i, v: (0, 0)),
+            ],
+            out_specs=pl.BlockSpec(
+                (blocks, 2, 2, 1, SUBLANES, count), lambda i, v: (0, 0, 0, i, 0, 0)
+            ),
+        ),
+        out_shape=jax.ShapeDtypeStruct(shape, F32),
+        compiler_params=pltpu.CompilerParams(vmem_limit_bytes=VMEM_LIMIT),
+        name="rows",
+    )(variant, arrived, first, turn, second)
+
+
+def band_kernel(taps_ref, o_ref):
+    half = LANES // 2
+    banded = []
+    for drift in range(2):
+        for part in range(2):
+            line = jnp.broadcast_to(taps_ref[0, 2 * drift + part : 2 * drift + part + 1, :], (half, LANES))
+            banded.append(pltpu.roll(line, 0, 1, stride=1, stride_axis=0))
+    re = jnp.concatenate([banded[0], banded[2]], axis=0)
+    im = jnp.concatenate([banded[1], banded[3]], axis=0)
+    lines = jnp.concatenate(
+        [jnp.concatenate([re, -im], axis=1), jnp.concatenate([im, re], axis=1)], axis=0
+    )
+    high, low = split(jnp.transpose(lines))
+    o_ref[0] = jnp.concatenate([high, low, high], axis=0)
+
+
+def band_stage(kernel_re, kernel_im):
+    drifts, taps = kernel_re.shape
+    lines = jnp.stack([kernel_re, kernel_im], axis=1)
+    lines = jnp.pad(lines, ((0, 0), (0, 0), (0, LANES - taps))).reshape(drifts // 2, 4, LANES)
+    return pl.pallas_call(
+        band_kernel,
+        grid=(drifts // 2,),
+        in_specs=[pl.BlockSpec((1, 4, LANES), lambda i: (i, 0, 0))],
+        out_specs=pl.BlockSpec((1, 6 * LANES, 2 * LANES), lambda i: (i, 0, 0)),
+        out_shape=jax.ShapeDtypeStruct((drifts // 2, 6 * LANES, 2 * LANES), BF16),
+        name="bands",
+    )(lines)
+
+
+def correlate_kernel(devices, slots, pad, x_ref, halo_ref, band_ref, o_ref, table, last, lhs):
+    step = pl.program_id(0)
+    steps = pl.num_programs(0)
+    total = 2 * devices * slots
+    pitch = total + pad
+    half = LANES // 2
+    taps_half = half // 2
+
+    @pl.when(step == 0)
+    def _():
+        def source(s, carry):
+            for side in range(2):
+                for part in range(2):
+                    for slot in range(slots):
+                        tile = x_ref[
+                            pl.ds(
+                                pl.multiple_of(
+                                    (((s * 2 + side) * 2 + part) * slots + slot) * SUBLANES, SUBLANES
+                                ),
+                                SUBLANES,
+                            ),
+                            :,
+                        ]
+                        row = s * slots + slot
+                        if side == 1:
+                            row = total - row
+                            if slot == 0:
+                                row = jnp.where(s == 0, total // 2, row)
+                        table[pl.ds(part * SUBLANES * pitch + row, SUBLANES, stride=pitch), :] = tile
+            return carry
+
+        lax.fori_loop(0, devices, source, 0)
+        last[...] = halo_ref[0:2, :]
+
+    lane = lax.broadcasted_iota(jnp.int32, (LANES, LANES), 1)
+    row_id = lax.broadcasted_iota(jnp.int32, (LANES, LANES), 0)
+    blocks = total // LANES
+
+    def turned(part, line, block):
+        start = pl.multiple_of((part * SUBLANES + line) * pitch + block * LANES, SUBLANES)
+        flat = jnp.transpose(table[pl.ds(start, LANES), :])
+        return pltpu.roll(flat, taps_half, 1)
+
+    next_line = jnp.minimum(step + 1, steps - 1)
+    for part in range(2):
+        rolled = [turned(part, step, block) for block in range(blocks)]
+        follow = turned(part, next_line, 0)[0:1, :]
+        follow = jnp.where(step == steps - 1, halo_ref[2 + part : 3 + part, :], follow)
+        before = jnp.where(row_id == 0, last[part : part + 1, :], pltpu.roll(rolled[-1], 1, 0))
+        after = jnp.where(row_id == LANES - 1, follow, pltpu.roll(rolled[0], LANES - 1, 0))
+        last[part : part + 1, :] = rolled[-1][LANES - 1 : LANES, :]
+        ext = []
+        for block in range(blocks + 1):
+            left = before if block == 0 else rolled[block - 1]
+            right = after if block == blocks else rolled[block]
+            ext.append(jnp.where(lane < taps_half, left, right))
+        for block in range(blocks):
+            odd = jnp.where(
+                lane < half, pltpu.roll(ext[block], half, 1), pltpu.roll(ext[block + 1], half, 1)
+            )
+            for parity, window in enumerate((ext[block], odd)):
+                high, low = split(window)
+                rows = pl.ds((2 * block + parity) * LANES, LANES)
+                lhs[rows, part * LANES : (part + 1) * LANES] = high
+                lhs[rows, (2 + part) * LANES : (3 + part) * LANES] = high
+                lhs[rows, (4 + part) * LANES : (5 + part) * LANES] = low
+
+    pairs = band_ref.shape[0]
+    group = 2
+    chunks = blocks // group
+
+    def multiply(index, carry):
+        pair = index // chunks
+        chunk = index % chunks
+        rows = pl.ds(pl.multiple_of(chunk * group * 2 * LANES, LANES), group * 2 * LANES)
+        out = jnp.dot(lhs[rows, :], band_ref[pair], preferred_element_type=F32)
+        power = out[:, :LANES] * out[:, :LANES] + out[:, LANES:] * out[:, LANES:]
+        outer = (2 * pair) // SUBLANES
+        inner = (2 * pair) % SUBLANES
+        for member in range(group):
+            even = power[member * 2 * LANES : (member * 2 + 1) * LANES]
+            odd = power[(member * 2 + 1) * LANES : (member * 2 + 2) * LANES]
+            values = (
+                jnp.where(lane < half, even, pltpu.roll(odd, half, 1)),
+                jnp.where(lane < half, pltpu.roll(even, half, 1), odd),
+            )
+            block = chunk * group + member
+            for drift, value in enumerate(values):
+                o_ref[
+                    outer,
+                    pl.ds(block * SUBLANES + inner + drift, LANES, stride=SUBLANES * blocks),
+                    :,
+                ] = value
+        return carry
+
+    lax.fori_loop(0, pairs * chunks, multiply, 0)
+
+
+def correlate_stage(arrived, halo, bands):
+    devices, _, _, slots, lines, count = arrived.shape
+    total = 2 * devices * slots
+    drifts = 2 * bands.shape[0]
+    groups = drifts // SUBLANES
+    pad = SUBLANES
+    flat = arrived.reshape(devices * 4 * slots * lines, count)
+    height = count * total // LANES * SUBLANES
+    out = pl.pallas_call(
+        functools.partial(correlate_kernel, devices, slots, pad),
+        grid=(lines,),
+        in_specs=[
+            pl.BlockSpec(flat.shape, lambda i: (0, 0), pipeline_mode=pl.Buffered(1)),
+            pl.BlockSpec(halo.shape, lambda i: (0, 0)),
+            pl.BlockSpec(bands.shape, lambda i: (0, 0, 0), pipeline_mode=pl.Buffered(1)),
+        ],
+        out_specs=pl.BlockSpec((groups, height, LANES), lambda i: (0, i, 0)),
+        out_shape=jax.ShapeDtypeStruct((groups, lines * height, LANES), F32),
+        scratch_shapes=[
+            pltpu.VMEM((2 * SUBLANES * (total + pad), LANES), F32),
+            pltpu.VMEM((2, LANES), F32),
+            pltpu.VMEM((2 * total // LANES * LANES, 6 * LANES), BF16),
+        ],
+        compiler_params=pltpu.CompilerParams(vmem_limit_bytes=VMEM_LIMIT),
+        name="correlate",
+    )(flat, halo, bands)
+    out = out.reshape(groups, lines * height // SUBLANES, SUBLANES, LANES)
+    return jnp.swapaxes(out, 1, 2).reshape(drifts, lines * height // SUBLANES * LANES)
+
+
+def halo_lines(arrived, taps):
+    half = taps // 2
+    devices, _, _, slots, lines, count = arrived.shape
+    total = 2 * devices * slots
+    first = arrived[:, 0, :, :, 0, 0]
+    final = arrived[:, 1, :, :, lines - 1, count - 1]
+    spread = lambda a: jnp.swapaxes(a, 0, 1).reshape(2, devices * slots)
+    head = spread(first)[:, :half]
+    tail = spread(final)[:, 1 : half + 1][:, ::-1]
+    size = lax.axis_size(AXES)
+    forward = [(i, i + 1) for i in range(size - 1)]
+    backward = [(i + 1, i) for i in range(size - 1)]
+    previous = lax.ppermute(tail, AXES, forward)
+    following = lax.ppermute(head, AXES, backward)
+    return jnp.concatenate(
+        [
+            jnp.pad(previous, ((0, 0), (0, LANES - half))),
+            jnp.pad(following, ((0, 0), (half, LANES - 2 * half))),
+        ],
+        axis=0,
+    )
+
+
+def tap_kernels(templates, drift_template, drift_reach):
+    taps = templates.shape[1] // 2
+    selector = (drift_template[:, None] == iota(templates.shape[0])[None, :]).astype(F32)
+    chosen = jnp.dot(
+        selector, templates, precision=lax.Precision.HIGHEST, preferred_element_type=F32
+    )
+    index = iota(taps)[None, :]
+    center = taps // 2
+    inside = (
+        (index >= center - drift_reach[:, None]) & (index < center + drift_reach[:, None])
+    ).astype(F32)
+    return chosen[:, :taps] * inside, chosen[:, taps:] * inside
+
+
+def fits(shape, devices, drifts, taps):
+    rows, cols = shape[1], shape[2]
+    lines = devices * cols // LANES
+    return (
+        2 * LANES // devices == SUBLANES
+        and lines // devices == SUBLANES
+        and rows % (2 * devices * SUBLANES) == 0
+        and drifts % SUBLANES == 0
+        and 2 * taps == LANES
+    )
+
+
+def local(series, templates, drift_template, drift_reach):
+    position = lax.axis_index(AXES)
+    devices = lax.axis_size(AXES)
+    rows, cols = series.shape[1], series.shape[2]
+    taps = templates.shape[1] // 2
+    if not fits(series.shape, devices, drift_template.shape[0], taps):
+        return general_local(series, templates, drift_template, drift_reach)
+    count = LANES
+    width = devices * cols // count
+    slots = rows // 2 // devices
+    samples = 2 * rows * cols * devices
+    bands = band_stage(*tap_kernels(templates, drift_template, drift_reach))
+    columns = column_stage(series, position, width)
+    columns = columns.reshape(devices, slots, 2 * width // LANES, SUBLANES, LANES)
+    arrived = lax.all_to_all(columns, AXES, 0, 0, tiled=True)
+    spectra = row_stage(arrived, position, rows, samples)
+    arrived = lax.all_to_all(spectra, AXES, 0, 0, tiled=True)
+    return correlate_stage(arrived, halo_lines(arrived, taps), bands)
 
 
 def solution(mesh):
     return jax.shard_map(
         local,
         mesh=mesh,
-        in_specs=(P(None, None, ("grp", "dev")), P(), P(), P()),
-        out_specs=P(None, ("grp", "dev")),
+        in_specs=(P(None, None, AXES), P(), P(), P()),
+        out_specs=P(None, AXES),
         check_vma=False,
     )

time: 1800 us -> 656 us (0.36)
  matrix products: 477 us -> 0.18 us
  local copies, waits for them, and re-layouts: 316 us -> 8.51 us
  blocking collectives: 280 us -> 0 us
  Pallas kernels: 0 us -> 238 us
  other arithmetic: 164 us -> 33.4 us
  starting transfers between devices: 118 us -> 20.2 us
  waiting for transfers between devices: 437 us -> 356 us
    dot_general x16 -> x1, matrix products: 477 us -> 0.18 us  [tap_kernels(): jnp.dot(selector, templates, precision=lax.Precision.HIGHEST, preferred_e...]
    all_to_all x2 -> x0, blocking collectives: 280 us -> none  [the longest x1 184 us: to_rows(): lax.all_to_all(shaped, 'grp', split_axis=1, concat_axis=4, tiled=True)]
    pallas_call x0 -> x4, Pallas kernels: none -> 238 us  [the longest x1 170 us: correlate_stage(): pl.pallas_call(functools.partial(correlate_kernel, devices, slots, pad),...]
    unnamed x30 -> x8, local copies, waits for them, and re-layouts: 82.2 us -> 0.02 us
    all_to_all x2, waiting for transfers between devices: 437 us -> 356 us  [the longest x1 185 us: local(): arrived = lax.all_to_all(spectra, AXES, 0, 0, tiled=True)]
    slice x12 -> x4, local copies, waits for them, and re-layouts: 72.7 us -> 5.12 us  [the longest x1 5.02 us: halo_lines(): final = arrived[:, 1, :, :, lines - 1, count - 1]]
    all_to_all x2, starting transfers between devices: 77.4 us -> 11 us  [the longest x1 6.16 us: local(): arrived = lax.all_to_all(columns, AXES, 0, 0, tiled=True)]
    add x3 -> x5, other arithmetic: 64.7 us -> 0.16 us  [the longest x1 0.07 us: column_stage(): 2 * (position * cols + width * iota(blocks)[:, None, None] + LANES * iota...]
  transfers between devices with their start and end apart: 4 -> 4, of which waited for: 2 -> 2; matrix products, arithmetic and copies ran while one was open for 1% -> 2% of each run, Pallas kernels for 0% -> 1%
where the time goes in v1:
time: 656 us
  waiting for transfers between devices  356 us (54%)
  Pallas kernels  238 us (36%)
  other arithmetic  33.4 us (5%)
  starting transfers between devices  20.2 us (3%)
  local copies, waits for them, and re-layouts  8.51 us (1%)
    all_to_all x1, waiting for transfers between devices, local(): arrived = lax.all_to_all(spectra, AXES, 0, 0, tiled=True)  185 us
    all_to_all x1, waiting for transfers between devices, local(): arrived = lax.all_to_all(columns, AXES, 0, 0, tiled=True)  171 us
    pallas_call x1, Pallas kernels, correlate_stage(): pl.pallas_call(functools.partial(correlate_kernel, devices, slots, pad),...  170 us
    pallas_call x1, Pallas kernels, row_stage(): pl.pallas_call(row_kernel, grid_spec=pltpu.PrefetchScalarGridSpec(num_sca...  35.6 us
    pallas_call x1, Pallas kernels, column_stage(): pl.pallas_call(column_kernel, grid=(blocks,), in_specs=[pl.BlockSpec((2,...  27.1 us
  transfers between devices with their start and end apart: 4, of which 2 were waited for; matrix products, arithmetic and copies ran while one was open for 2% of the time, Pallas kernels for 1%

profile of v1, /device:TPU:4, one launch (start us, length us, event | category | flops | bytes accessed | tf_op | source)
XLA Modules:
  0.0 656.1 jit_solution(5399406341327691612)
XLA Ops:
  0.1 0.1 add.569
  0.2 0.1 add_multiply_fusion
  0.2 0.1 broadcast_add_fusion
  0.3 0.1 copy.23
  0.4 0.1 fusion.61
  0.5 0.2 fusion.78
  0.7 1.8 fusion.49
  2.5 0.4 copy.24
  2.9 4.5 multiply_sine_fusion
  7.4 1.1 subtract_dynamic-update-slice_fusion.7
  8.5 1.1 subtract_dynamic-update-slice_fusion.6
  9.6 1.1 subtract_dynamic-update-slice_fusion.5
  10.7 1.1 subtract_dynamic-update-slice_fusion.4
  11.8 1.1 subtract_dynamic-update-slice_fusion.3
  12.9 1.1 subtract_dynamic-update-slice_fusion.2
  14.0 1.1 subtract_dynamic-update-slice_fusion.1
  15.1 1.1 subtract_dynamic-update-slice_fusion
  16.2 0.2 negate_select_fusion
  16.4 0.9 reduce-precision_convert_fusion
  17.4 2.4 pad_maximum_fusion.1.table_ref
  19.8 27.1 %columns.1 = f32[16384,128]{1,0:T(8,128)} custom-call(f32[2,1024,1024]{2,1,0:T(8,128)} %x_ref.1, bf16[1024,2048]{1,0:T(8,128)(2,1)} %pad_maximum_fusion.1.table_ref, f32[512,128]{1,0:T(8,128)} %get-tuple-element.84.base_re_ref, f32[512,128]{1,0:T(8,128)} %get-tuple-element.83.base_im_ref, f32[4,512,4]{2,1,0:T(8,128)} %get-tuple-element.14.step_re_ref, ...), custom_call_target="tpu_custom_call" | custom-call | tf_op jit(solution)/shard_map/columns/pallas_call | solution.py:309
  46.8 6.2 all-to-all-start
  53.1 0.1 iota_add_fusion
  53.1 1.7 fusion.62
  54.9 0.1 copy.32
  55.0 0.1 copy.31
  55.1 0.1 pad_maximum_fusion.8
  55.3 0.1 copy.25
  55.4 0.1 copy.29
  55.5 0.1 copy.26
  55.6 0.1 copy.30
  55.7 0.1 copy.28
  55.8 0.1 copy.27
  55.9 0.6 and_select_fusion.variant_ref
  56.5 3.1 fusion.46
  59.7 0.2 fusion.7
  59.9 0.1 maximum_bitcast_fusion.2
  60.0 1.3 pad_maximum_fusion.4.first_ref
  61.3 0.3 fusion.4
  61.5 1.6 pad_maximum_fusion.3.turn_ref
  63.2 2.1 fusion.29
  65.3 0.4 fusion.3
  65.7 1.8 pad_maximum_fusion.2.second_ref
  67.5 170.7 %all-to-all-done.x_ref = f32[32,16,4,8,128]{4,3,2,1,0:T(8,128)} async-done(((f32[32,16,4,8,128]{4,3,2,1,0:T(8,128)}), f32[32,16,4,8,128]{4,3,2,1,0:T(8,128)}, u32[]{:S(2)}, u32[]{:S(2)}) %all-to-all-start) | async-done | bytes 8388640 | tf_op jit(solution)/shard_map/all_to_all | solution.py:635
  238.2 35.6 %rows.1 = f32[32,2,2,16,8,128]{5,4,3,2,1,0:T(8,128)} custom-call(s32[16]{0:T(128)} %and_select_fusion.variant_ref, f32[32,16,4,8,128]{4,3,2,1,0:T(8,128)} %all-to-all-done.x_ref, bf16[2,512,768]{2,1,0:T(8,128)(2,1)} %pad_maximum_fusion.4.first_ref, f32[2,2,2,128,512]{4,3,2,1,0:T(8,128)} %pad_maximum_fusion.3.turn_ref, ...), custom_call_target="tpu_custom_call" | custom-call | tf_op jit(solution)/shard_map/rows/pallas_call | solution.py:393
  273.9 4.9 all-to-all-start.1
  278.8 0.2 fusion.72
  279.0 0.1 fusion.75
  279.1 185.0 %all-to-all-done.1 = f32[32,2,2,16,8,128]{5,4,3,2,1,0:T(8,128)} async-done(((f32[32,2,2,16,8,128]{5,4,3,2,1,0:T(8,128)}), f32[32,2,2,16,8,128]{5,4,3,2,1,0:T(8,128)}, u32[]{:S(2)}, u32[]{:S(2)}) %all-to-all-start.1) | async-done | bytes 8388640 | tf_op jit(solution)/shard_map/all_to_all | solution.py:637
  464.1 5.0 fusion.87
  469.1 0.6 copy.38
  469.7 0.1 reshape.727
  469.8 0.1 slice.153
  469.9 0.1 rev.3
  470.0 1.9 collective-permute-start
  471.9 0.6 copy.39
  472.4 0.1 reshape.728
  472.6 7.2 %collective-permute-start.1 = (f32[2,32]{1,0:T(2,128)S(1)}, f32[2,32]{1,0:T(2,128)S(1)}, u32[]{:S(2)}, u32[]{:S(2)}) collective-permute-start(f32[2,32]{1,0:T(2,128)S(1)} %slice.155), channel_id=1, source_target_pairs={{1,0},{2,1},{3,2},{4,3},{5,4},{6,5},{7,6},{8,7},{9,8},{10,9},{11,1... | collective-permute-start | bytes 776 | tf_op jit(solution)/shard_map/ppermute | solution.py:585
  479.8 0.6 pad.18.clone
  480.4 5.3 bands.1.band_ref
  485.7 0.0 collective-permute-done
  485.7 0.0 collective-permute-done.1
  485.7 0.7 select_maximum_fusion.halo_ref
  486.4 169.7 %correlate.1 = f32[2,65536,128]{2,1,0:T(8,128)} custom-call(f32[16384,128]{1,0:T(8,128)} %bitcast.33.x_ref, f32[4,128]{1,0:T(4,128)} %select_maximum_fusion.halo_ref, bf16[8,768,256]{2,1,0:T(8,128)(2,1)} %bands.1.band_ref), custom_call_target="tpu_custom_call" | custom-call | tf_op jit(solution)/shard_map/correlate/pallas_call | solution.py:550
  (30 shorter events, 0.3 us)
Async XLA Ops:
  0.0 278.8 %copy-start = (f32[200,128]{1,0:T(8,128)S(1)}, f32[200,128]{1,0:T(8,128)}, u32[]{:S(2)}) copy-start(f32[200,128]{1,0:T(8,128)} %param.5) | copy-start | bytes 307204
  46.8 191.4 %all-to-all-start = ((f32[32,16,4,8,128]{4,3,2,1,0:T(8,128)}), f32[32,16,4,8,128]{4,3,2,1,0:T(8,128)}, u32[]{:S(2)}, u32[]{:S(2)}) async-start(f32[32,16,4,8,128]{4,3,2,1,0:T(8,128)} %bitcast.61), calls=%async_computation | async-start | bytes 16777216 | tf_op jit(solution)/shard_map/all_to_all | solution.py:635
  273.9 4.9 copy-start.2
  273.9 4.9 copy-start.1
  273.9 190.2 %all-to-all-start.1 = ((f32[32,2,2,16,8,128]{5,4,3,2,1,0:T(8,128)}), f32[32,2,2,16,8,128]{5,4,3,2,1,0:T(8,128)}, u32[]{:S(2)}, u32[]{:S(2)}) async-start(f32[32,2,2,16,8,128]{5,4,3,2,1,0:T(8,128)} %rows.1), calls=%async_computation.1 | async-start | bytes 16777216 | tf_op jit(solution)/shard_map/all_to_all | solution.py:637
  470.0 15.8 %collective-permute-start = (f32[2,32]{1,0:T(2,128)S(1)}, f32[2,32]{1,0:T(2,128)S(1)}, u32[]{:S(2)}, u32[]{:S(2)}) collective-permute-start(f32[2,32]{1,0:T(2,128)S(1)} %rev.3), channel_id=1, source_target_pairs={{0,1},{1,2},{2,3},{3,4},{4,5},{5,6},{6,7},{7,8},{8,9},{9,10},{10,1... | collective-permute-start | bytes 776 | tf_op jit(solution)/shard_map/ppermute | solution.py:584
  472.6 13.2 %collective-permute-start.1 = (f32[2,32]{1,0:T(2,128)S(1)}, f32[2,32]{1,0:T(2,128)S(1)}, u32[]{:S(2)}, u32[]{:S(2)}) collective-permute-start(f32[2,32]{1,0:T(2,128)S(1)} %slice.155), channel_id=1, source_target_pairs={{1,0},{2,1},{3,2},{4,3},{5,4},{6,5},{7,6},{8,7},{9,8},{10,9},{11,1... | collective-permute-start | bytes 776 | tf_op jit(solution)/shard_map/ppermute | solution.py:585

commit v2 on v1

--- a/solution.py
+++ b/solution.py
@@ -8,10 +8,12 @@
 from jax.experimental.pallas import tpu as pltpu
 from jax.sharding import PartitionSpec as P
 
+
 AXES = ("grp", "dev")
 LANES = 128
 SUBLANES = 8
 VMEM_LIMIT = 60 * 1024 * 1024
+PARTS = 2
 F32 = jnp.float32
 BF16 = jnp.bfloat16
 
@@ -251,80 +253,100 @@
     return correlate(extended, kernels, segment_bins)
 
 
-def column_kernel(x_ref, table_ref, base_re_ref, base_im_ref, step_re_ref, step_im_ref, o_ref):
+def column_kernel(packed, *refs):
+    inner = SUBLANES // 2
+    x_refs, refs = refs[:inner], refs[inner:]
+    near_re_ref, near_im_ref, far_re_ref, far_im_ref = refs[:4]
+    base_re_ref, base_im_ref, step_re_ref, step_im_ref, o_ref, table, stage = refs[4:]
     slots = base_re_ref.shape[0]
-    rows = x_ref.shape[1]
-    width = x_ref.shape[2]
-    block = pl.program_id(0)
-    blocks = pl.num_programs(0)
-    x = jnp.concatenate([x_ref[0], x_ref[1]], axis=1)
-    high, low = split(x)
+    rows = x_refs[0].shape[1]
+    span = slots + SUBLANES
+
+    @pl.when(pl.program_id(0) == 0)
+    def _():
+        near_re = near_re_ref[...]
+        near_im = near_im_ref[...]
+        slot = lax.broadcasted_iota(jnp.int32, (slots, LANES), 0)
+        lane = lax.broadcasted_iota(jnp.int32, (slots, LANES), 1)
+        alternating = jnp.where(lane % 2 == 0, 1.0, -1.0).astype(F32)
+        for block in range(rows // LANES):
+            far_re = far_re_ref[:, block : block + 1]
+            far_im = far_im_ref[:, block : block + 1]
+            cos = near_re * far_re - near_im * far_im
+            sin = near_re * far_im + near_im * far_re
+            sin = jnp.where(slot == 0, alternating, -sin) if packed else -sin
+            for part, value in enumerate((cos, sin)):
+                high, low = split(value)
+                lines = slice(part * slots, (part + 1) * slots)
+                table[lines, block * LANES : (block + 1) * LANES] = high
+                table[lines, rows + block * LANES : rows + (block + 1) * LANES] = low
+
+    high, low = split(jnp.concatenate([r[0] for r in x_refs], axis=1))
     out = jnp.dot(
-        table_ref[...], jnp.concatenate([high, high], axis=0), preferred_element_type=F32
-    ) + jnp.dot(table_ref[:, :rows], low, preferred_element_type=F32)
+        table[...], jnp.concatenate([high, high], axis=0), preferred_element_type=F32
+    ) + jnp.dot(table[:, :rows], low, preferred_element_type=F32)
     base_re = base_re_ref[...]
     base_im = base_im_ref[...]
-    for chunk in range(2 * width // LANES):
-        lanes = slice(chunk * LANES, (chunk + 1) * LANES)
-        step_re = step_re_ref[0, :, chunk : chunk + 1]
-        step_im = step_im_ref[0, :, chunk : chunk + 1]
+    for block in range(inner):
+        lanes = slice(block * LANES, (block + 1) * LANES)
+        step_re = step_re_ref[0, :, block : block + 1]
+        step_im = step_im_ref[0, :, block : block + 1]
         turn_re = base_re * step_re - base_im * step_im
         turn_im = base_re * step_im + base_im * step_re
         real = out[:slots, lanes]
         imag = out[slots:, lanes]
-        pitch = 2 * width // LANES * SUBLANES
-        start = chunk * SUBLANES + block
-        o_ref[pl.ds(start, slots, stride=pitch), :] = real * turn_re + imag * turn_im
-        o_ref[pl.ds(start + blocks, slots, stride=pitch), :] = imag * turn_re - real * turn_im
-
-
-def column_stage(series, position, width):
+        stage[block * span : block * span + slots, :] = real * turn_re + imag * turn_im
+        start = (inner + block) * span
+        stage[start : start + slots, :] = imag * turn_re - real * turn_im
+    for slot in range(slots):
+        o_ref[slot, 0] = stage[pl.ds(slot, SUBLANES, stride=span), :]
+
+
+def column_stage(series, position, width, part):
     rows, cols = series.shape[1], series.shape[2]
-    slots = rows // 2
-    blocks = cols // width
+    slots = rows // 2 // PARTS
+    inner = cols // width
+    chunks = width // LANES
     samples = 2 * rows * cols * lax.axis_size(AXES)
-    slot = iota(slots)
+    slot = part * slots + iota(slots)
     near_re, near_im = phases(slot[:, None] * iota(LANES)[None, :], rows)
     far_re, far_im = phases(slot[:, None] * (LANES * iota(rows // LANES))[None, :], rows)
-    cos = jnp.concatenate(
-        [near_re * far_re[:, i : i + 1] - near_im * far_im[:, i : i + 1] for i in range(rows // LANES)],
-        axis=1,
-    )
-    sin = jnp.concatenate(
-        [near_re * far_im[:, i : i + 1] + near_im * far_re[:, i : i + 1] for i in range(rows // LANES)],
-        axis=1,
-    )
-    alternating = (1 - 2 * (iota(rows) % 2)).astype(F32)[None, :]
-    sin = jnp.where(slot[:, None] == 0, alternating, -sin)
-    table = jnp.concatenate(split_xla(jnp.concatenate([cos, sin], axis=0)), axis=1)
     base_re, base_im = phases(slot[:, None] * (2 * iota(LANES))[None, :], samples)
-    chunks = width // LANES
     start = (
-        2 * (position * cols + width * iota(blocks)[:, None, None] + LANES * iota(chunks)[None, None, :])
-        + iota(2)[None, :, None]
-    ).reshape(blocks, 1, 2 * chunks)
-    step_re, step_im = phases(start * slot[None, :, None], samples)
-    small = pl.BlockSpec((1, slots, 2 * chunks), lambda i: (i, 0, 0))
+        2 * (position * cols + width * iota(inner)[None, None, :] + LANES * iota(chunks)[None, :, None])
+        + iota(2)[:, None, None]
+    ).reshape(2 * chunks * inner, 1)
+    steps = [
+        jnp.swapaxes(a.reshape(2 * chunks, inner, slots), 1, 2)
+        for a in phases(start * slot[None, :], samples)
+    ]
+    small = pl.BlockSpec((1, slots, inner), lambda i: (i, 0, 0))
     whole = lambda a: pl.BlockSpec(a.shape, lambda i: (0, 0))
+    column = lambda block: pl.BlockSpec(
+        (1, rows, LANES), lambda i: (i // chunks, 0, block * chunks + i % chunks)
+    )
+    tables = (near_re, near_im, far_re, far_im, base_re, base_im)
     return pl.pallas_call(
-        column_kernel,
-        grid=(blocks,),
-        in_specs=[
-            pl.BlockSpec((2, rows, width), lambda i: (0, 0, i)),
-            whole(table),
-            whole(base_re),
-            whole(base_im),
-            small,
-            small,
+        functools.partial(column_kernel, part == 0),
+        grid=(2 * chunks,),
+        in_specs=[column(block) for block in range(inner)]
+        + [whole(table) for table in tables]
+        + [small, small],
+        out_specs=pl.BlockSpec((slots, 1, SUBLANES, LANES), lambda i: (0, i, 0, 0)),
+        out_shape=jax.ShapeDtypeStruct((slots, 2 * chunks, SUBLANES, LANES), F32),
+        scratch_shapes=[
+            pltpu.VMEM((2 * slots, 2 * rows), BF16),
+            pltpu.VMEM(((SUBLANES + 1) * (slots + SUBLANES), LANES), F32),
         ],
-        out_specs=pl.BlockSpec((slots * 2 * chunks * SUBLANES, LANES), lambda i: (0, 0)),
-        out_shape=jax.ShapeDtypeStruct((slots * 2 * chunks * SUBLANES, LANES), F32),
         compiler_params=pltpu.CompilerParams(vmem_limit_bytes=VMEM_LIMIT),
+        cost_estimate=pl.CostEstimate(
+            flops=24 * slots * rows * cols, transcendentals=0, bytes_accessed=12 * rows * cols
+        ),
         name="columns",
-    )(series, table, base_re, base_im, step_re, step_im)
-
-
-def row_kernel(variant_ref, x_ref, first_ref, turn_ref, second_ref, o_ref):
+    )(*[series] * inner, *tables, *steps)
+
+
+def row_kernel(variant_ref, x_ref, first_ref, turn_ref, second_ref, *o_refs):
     depth = first_ref.shape[2] // 3
     count, width = turn_ref.shape[3], turn_ref.shape[4]
     x = [x_ref[:, 0, i].reshape(depth, LANES) for i in range(width // LANES)]
@@ -349,15 +371,16 @@
         (((1,), (1,)), ((), ())),
         preferred_element_type=F32,
     )
-    half = result.shape[0] // 2
-    for side in range(2):
-        for part in range(2):
-            block = result[part * half : (part + 1) * half, side * count : (side + 1) * count]
-            o_ref[:, side, part, 0] = block.reshape(half // SUBLANES, SUBLANES, count)
-
-
-def row_stage(arrived, position, total_rows, samples):
-    devices, slots, chunks, sublanes, _ = arrived.shape
+    height = result.shape[0] // len(o_refs)
+    for index, o_ref in enumerate(o_refs):
+        for side in range(2):
+            block = result[
+                index * height : (index + 1) * height, side * count : (side + 1) * count
+            ]
+            o_ref[:, side, 0] = block.reshape(height // SUBLANES, SUBLANES, count)
+
+
+def row_tables(devices, chunks, sublanes, samples):
     width = chunks * LANES
     inner = sublanes // 2
     count = devices * inner
@@ -381,15 +404,33 @@
     turn_b = jnp.stack(phases((freq + 1) * beta, length))
     turn_c = jnp.stack(phases((2 * freq + 1) * beta, 2 * length))
     turn = jnp.stack([jnp.stack([turn_a, turn_b]), jnp.stack([turn_a, turn_c])])
-    gc, gs = phases(iota(lines)[:, None] * beta, width)
-    second = jnp.concatenate(
-        [jnp.concatenate([gc, gs], axis=1), jnp.concatenate([-gs, gc], axis=1)], axis=0
-    ) * (1.0 / math.sqrt(samples))
+    inside = SUBLANES // 2
+    line = (
+        SUBLANES * iota(devices)[None, :, None]
+        + inside * iota(PARTS)[:, None, None]
+        + iota(inside)[None, None, :]
+    )
+    gc, gs = [
+        a.reshape(PARTS, devices, inside, width)
+        for a in phases(line.reshape(lines, 1) * beta, width)
+    ]
+    second = jnp.stack(
+        [jnp.concatenate([gc, gs], axis=3), jnp.concatenate([-gs, gc], axis=3)], axis=2
+    ).reshape(2 * lines, 2 * width) * (1.0 / math.sqrt(samples))
     high, low = split_xla(second)
     second = jnp.concatenate([high, low, high], axis=1)
+    return first, turn, second
+
+
+def row_stage(arrived, tables, position, part):
+    devices, slots, chunks, sublanes, _ = arrived.shape
+    first, turn, second = tables
+    count = turn.shape[4 - 1]
     variant = jnp.where((iota(slots) == 0) & (position == 0), 1, 0).astype(jnp.int32)
-    blocks = lines // SUBLANES
-    shape = (blocks, 2, 2, slots, SUBLANES, count)
+    if part > 0:
+        variant = jnp.zeros((slots,), jnp.int32)
+    blocks = second.shape[0] // PARTS // SUBLANES
+    shape = (blocks, 2, slots, SUBLANES, count)
     return pl.pallas_call(
         row_kernel,
         grid_spec=pltpu.PrefetchScalarGridSpec(
@@ -401,12 +442,18 @@
                 pl.BlockSpec((1,) + turn.shape[1:], lambda i, v: (v[i], 0, 0, 0, 0)),
                 pl.BlockSpec(second.shape, lambda i, v: (0, 0)),
             ],
-            out_specs=pl.BlockSpec(
-                (blocks, 2, 2, 1, SUBLANES, count), lambda i, v: (0, 0, 0, i, 0, 0)
-            ),
+            out_specs=[
+                pl.BlockSpec((blocks, 2, 1, SUBLANES, count), lambda i, v: (0, 0, i, 0, 0))
+                for _ in range(PARTS)
+            ],
         ),
-        out_shape=jax.ShapeDtypeStruct(shape, F32),
+        out_shape=[jax.ShapeDtypeStruct(shape, F32) for _ in range(PARTS)],
         compiler_params=pltpu.CompilerParams(vmem_limit_bytes=VMEM_LIMIT),
+        cost_estimate=pl.CostEstimate(
+            flops=slots * 2 * (first.shape[1] * first.shape[2] * chunks * LANES + 2 * count * second.size),
+            transcendentals=0,
+            bytes_accessed=8 * arrived.size,
+        ),
         name="rows",
     )(variant, arrived, first, turn, second)
 
@@ -441,10 +488,15 @@
     )(lines)
 
 
-def correlate_kernel(devices, slots, pad, x_ref, halo_ref, band_ref, o_ref, table, last, lhs):
+def correlate_kernel(
+    devices, slots, pad, inputs, *refs
+):
+    x_refs, (halo_ref, band_ref) = refs[:inputs], refs[inputs : inputs + 2]
+    o_ref, table, last, lhs, stage_a, stage_b = refs[-6:]
     step = pl.program_id(0)
     steps = pl.num_programs(0)
-    total = 2 * devices * slots
+    inside = SUBLANES // 2
+    total = 2 * PARTS * devices * slots
     pitch = total + pad
     half = LANES // 2
     taps_half = half // 2
@@ -452,24 +504,20 @@
     @pl.when(step == 0)
     def _():
         def source(s, carry):
-            for side in range(2):
-                for part in range(2):
+            for part in range(PARTS):
+                for side in range(2):
                     for slot in range(slots):
-                        tile = x_ref[
-                            pl.ds(
-                                pl.multiple_of(
-                                    (((s * 2 + side) * 2 + part) * slots + slot) * SUBLANES, SUBLANES
-                                ),
-                                SUBLANES,
-                            ),
-                            :,
-                        ]
-                        row = s * slots + slot
+                        x_ref = x_refs[min(part, inputs - 1)]
+                        tiles = x_ref.shape[0] // devices // SUBLANES
+                        place = (part * 2 + side if inputs < PARTS else side) * slots + slot
+                        start = (s * tiles + place) * SUBLANES
+                        tile = x_ref[pl.ds(pl.multiple_of(start, SUBLANES), SUBLANES), :]
+                        row = (part * devices + s) * slots + slot
                         if side == 1:
                             row = total - row
-                            if slot == 0:
+                            if slot == 0 and part == 0:
                                 row = jnp.where(s == 0, total // 2, row)
-                        table[pl.ds(part * SUBLANES * pitch + row, SUBLANES, stride=pitch), :] = tile
+                        table[pl.ds(row, SUBLANES, stride=pitch), :] = tile
             return carry
 
         lax.fori_loop(0, devices, source, 0)
@@ -480,7 +528,7 @@
     blocks = total // LANES
 
     def turned(part, line, block):
-        start = pl.multiple_of((part * SUBLANES + line) * pitch + block * LANES, SUBLANES)
+        start = pl.multiple_of((part * inside + line) * pitch + block * LANES, SUBLANES)
         flat = jnp.transpose(table[pl.ds(start, LANES), :])
         return pltpu.roll(flat, taps_half, 1)
 
@@ -508,88 +556,120 @@
                 lhs[rows, (2 + part) * LANES : (3 + part) * LANES] = high
                 lhs[rows, (4 + part) * LANES : (5 + part) * LANES] = low
 
-    pairs = band_ref.shape[0]
     group = 2
     chunks = blocks // group
-
-    def multiply(index, carry):
-        pair = index // chunks
-        chunk = index % chunks
+    drifts = SUBLANES
+    span = LANES + SUBLANES
+
+    def multiply(chunk, outer, target):
         rows = pl.ds(pl.multiple_of(chunk * group * 2 * LANES, LANES), group * 2 * LANES)
-        out = jnp.dot(lhs[rows, :], band_ref[pair], preferred_element_type=F32)
-        power = out[:, :LANES] * out[:, :LANES] + out[:, LANES:] * out[:, LANES:]
-        outer = (2 * pair) // SUBLANES
-        inner = (2 * pair) % SUBLANES
+        windows = lhs[rows, :]
+        for pair in range(drifts // 2):
+            out = jnp.dot(
+                windows, band_ref[outer * drifts // 2 + pair], preferred_element_type=F32
+            )
+            power = out[:, :LANES] * out[:, :LANES] + out[:, LANES:] * out[:, LANES:]
+            for member in range(group):
+                even = power[member * 2 * LANES : (member * 2 + 1) * LANES]
+                odd = power[(member * 2 + 1) * LANES : (member * 2 + 2) * LANES]
+                start = (member * drifts + 2 * pair) * span
+                target[start : start + LANES, :] = jnp.where(lane < half, even, pltpu.roll(odd, half, 1))
+                start += span
+                target[start : start + LANES, :] = jnp.where(lane < half, pltpu.roll(even, half, 1), odd)
+
+    def emit(chunk, outer, origin):
         for member in range(group):
-            even = power[member * 2 * LANES : (member * 2 + 1) * LANES]
-            odd = power[(member * 2 + 1) * LANES : (member * 2 + 2) * LANES]
-            values = (
-                jnp.where(lane < half, even, pltpu.roll(odd, half, 1)),
-                jnp.where(lane < half, pltpu.roll(even, half, 1), odd),
-            )
-            block = chunk * group + member
-            for drift, value in enumerate(values):
-                o_ref[
-                    outer,
-                    pl.ds(block * SUBLANES + inner + drift, LANES, stride=SUBLANES * blocks),
-                    :,
-                ] = value
+            for line in range(LANES):
+                value = origin[pl.ds(member * drifts * span + line, drifts, stride=span), :]
+                start = (line * blocks + member + chunk * group) * SUBLANES
+                o_ref[outer, pl.ds(pl.multiple_of(start, SUBLANES), SUBLANES), :] = value
+
+    groups = o_ref.shape[0]
+    stages = (stage_a, stage_b)
+
+    def body(chunk, carry):
+        for outer in range(groups):
+            multiply(chunk, outer, stages[outer % 2])
+            if outer == 0:
+                emit(jnp.maximum(chunk - 1, 0), groups - 1, stages[(groups - 1) % 2])
+            else:
+                emit(chunk, outer - 1, stages[(outer - 1) % 2])
         return carry
 
-    lax.fori_loop(0, pairs * chunks, multiply, 0)
-
-
-def correlate_stage(arrived, halo, bands):
-    devices, _, _, slots, lines, count = arrived.shape
-    total = 2 * devices * slots
+    lax.fori_loop(0, chunks, body, 0)
+    emit(chunks - 1, groups - 1, stages[(groups - 1) % 2])
+
+
+def correlate_stage(arrived, halo, bands, part, earlier, slots):
+    devices, _, _, count = arrived[0].shape
+    total = 2 * PARTS * devices * slots
     drifts = 2 * bands.shape[0]
     groups = drifts // SUBLANES
     pad = SUBLANES
-    flat = arrived.reshape(devices * 4 * slots * lines, count)
+    inside = SUBLANES // 2
+    flat = [a.reshape(-1, count) for a in arrived]
     height = count * total // LANES * SUBLANES
-    out = pl.pallas_call(
-        functools.partial(correlate_kernel, devices, slots, pad),
-        grid=(lines,),
-        in_specs=[
-            pl.BlockSpec(flat.shape, lambda i: (0, 0), pipeline_mode=pl.Buffered(1)),
-            pl.BlockSpec(halo.shape, lambda i: (0, 0)),
-            pl.BlockSpec(bands.shape, lambda i: (0, 0, 0), pipeline_mode=pl.Buffered(1)),
-        ],
-        out_specs=pl.BlockSpec((groups, height, LANES), lambda i: (0, i, 0)),
-        out_shape=jax.ShapeDtypeStruct((groups, lines * height, LANES), F32),
+    resident = lambda shape: pl.BlockSpec(
+        shape, lambda i: (0,) * len(shape), pipeline_mode=pl.Buffered(1)
+    )
+    extra = [] if earlier is None else [earlier]
+    return pl.pallas_call(
+        functools.partial(correlate_kernel, devices, slots, pad, len(flat)),
+        grid=(inside,),
+        in_specs=[resident(a.shape) for a in flat]
+        + [resident(halo.shape), resident(bands.shape)]
+        + [pl.BlockSpec(memory_space=pl.ANY) for _ in extra],
+        out_specs=pl.BlockSpec((groups, height, LANES), lambda i: (0, part * inside + i, 0)),
+        out_shape=jax.ShapeDtypeStruct((groups, PARTS * inside * height, LANES), F32),
+        input_output_aliases={} if earlier is None else {len(flat) + 2: 0},
         scratch_shapes=[
-            pltpu.VMEM((2 * SUBLANES * (total + pad), LANES), F32),
+            pltpu.VMEM(((SUBLANES + 1) * (total + pad), LANES), F32),
             pltpu.VMEM((2, LANES), F32),
             pltpu.VMEM((2 * total // LANES * LANES, 6 * LANES), BF16),
+            pltpu.VMEM(((2 * SUBLANES + 1) * (LANES + SUBLANES), LANES), F32),
+            pltpu.VMEM(((2 * SUBLANES + 1) * (LANES + SUBLANES), LANES), F32),
         ],
         compiler_params=pltpu.CompilerParams(vmem_limit_bytes=VMEM_LIMIT),
+        cost_estimate=pl.CostEstimate(
+            flops=inside * 12 * bands.shape[0] * total * count * LANES * 2 // 8,
+            transcendentals=0,
+            bytes_accessed=groups * inside * height * LANES * 4,
+        ),
         name="correlate",
-    )(flat, halo, bands)
-    out = out.reshape(groups, lines * height // SUBLANES, SUBLANES, LANES)
-    return jnp.swapaxes(out, 1, 2).reshape(drifts, lines * height // SUBLANES * LANES)
-
-
-def halo_lines(arrived, taps):
+    )(*flat, halo, bands, *extra)
+
+
+def edge_lines(spectra):
+    low, high = spectra
+    devices, _, slots, sublanes, count = low.shape
+    inside = sublanes // 2
+    first = lambda a: a[:, 0, :, ::inside, 0]
+    final = lambda a: a[:, 1, :, inside - 1 :: inside, count - 1]
+    blank = jnp.zeros_like(first(low)[:1])
+    edges = jnp.stack(
+        [
+            jnp.concatenate([blank, final(high)[:-1]]),
+            first(high),
+            final(low),
+            jnp.concatenate([first(low)[1:], blank]),
+        ],
+        axis=1,
+    )
+    edges = jnp.moveaxis(edges, 3, 2).reshape(devices, 1, 8, slots)
+    return jnp.pad(edges, ((0, 0), (0, 0), (0, 0), (0, count - slots)))
+
+
+def halo_lines(edges, slots, taps):
     half = taps // 2
-    devices, _, _, slots, lines, count = arrived.shape
-    total = 2 * devices * slots
-    first = arrived[:, 0, :, :, 0, 0]
-    final = arrived[:, 1, :, :, lines - 1, count - 1]
-    spread = lambda a: jnp.swapaxes(a, 0, 1).reshape(2, devices * slots)
-    head = spread(first)[:, :half]
-    tail = spread(final)[:, 1 : half + 1][:, ::-1]
-    size = lax.axis_size(AXES)
-    forward = [(i, i + 1) for i in range(size - 1)]
-    backward = [(i + 1, i) for i in range(size - 1)]
-    previous = lax.ppermute(tail, AXES, forward)
-    following = lax.ppermute(head, AXES, backward)
-    return jnp.concatenate(
-        [
-            jnp.pad(previous, ((0, 0), (0, LANES - half))),
-            jnp.pad(following, ((0, 0), (half, LANES - 2 * half))),
-        ],
-        axis=0,
-    )
+    devices = edges.shape[0]
+    lines = jnp.moveaxis(edges[:, :, :slots].reshape(devices, 4, 2, slots), 0, 2)
+    lines = lines.reshape(4, 2, devices * slots)
+    tail = lambda a: jnp.pad(a[:, half:0:-1], ((0, 0), (0, LANES - half)))
+    head = lambda a: jnp.pad(a[:, :half], ((0, 0), (half, LANES - 2 * half)))
+    return [
+        jnp.concatenate([tail(lines[2 * part]), head(lines[2 * part + 1])], axis=0)
+        for part in range(PARTS)
+    ]
 
 
 def tap_kernels(templates, drift_template, drift_reach):
@@ -625,17 +705,36 @@
     taps = templates.shape[1] // 2
     if not fits(series.shape, devices, drift_template.shape[0], taps):
         return general_local(series, templates, drift_template, drift_reach)
-    count = LANES
-    width = devices * cols // count
-    slots = rows // 2 // devices
+    width = devices * cols // LANES
+    slots = rows // 2 // devices // PARTS
     samples = 2 * rows * cols * devices
+    chunks = 2 * width // LANES
+    arrived = []
+    swap = lambda value: lax.all_to_all(value, AXES, 0, 0, tiled=True)
+    tables = row_tables(devices, chunks, SUBLANES, samples)
     bands = band_stage(*tap_kernels(templates, drift_template, drift_reach))
-    columns = column_stage(series, position, width)
-    columns = columns.reshape(devices, slots, 2 * width // LANES, SUBLANES, LANES)
-    arrived = lax.all_to_all(columns, AXES, 0, 0, tiled=True)
-    spectra = row_stage(arrived, position, rows, samples)
-    arrived = lax.all_to_all(spectra, AXES, 0, 0, tiled=True)
-    return correlate_stage(arrived, halo_lines(arrived, taps), bands)
+    for part in range(PARTS):
+        columns = column_stage(series, position, width, part)
+        columns = columns.reshape(devices, slots, chunks, SUBLANES, LANES)
+        if part == PARTS - 1:
+            columns, tables, bands = lax.optimization_barrier((columns, tables, bands))
+        arrived.append(swap(columns))
+    pieces = []
+    for part in range(PARTS):
+        spectra = row_stage(arrived[part], tables, position, part)
+        tiles = [a.reshape(devices, 2 * slots, SUBLANES, LANES) for a in spectra]
+        if part == 0:
+            tiles[0] = jnp.concatenate([tiles[0], edge_lines(spectra)], axis=1)
+        pieces.append(tiles)
+    first = swap(pieces[0][0])
+    second = swap(pieces[1][0])
+    rest = swap(jnp.concatenate([pieces[0][1], pieces[1][1]], axis=1))
+    halos = halo_lines(first[:, 2 * slots], slots, taps)
+    out = correlate_stage([first, second], halos[0], bands, 0, None, slots)
+    out = correlate_stage([rest], halos[1], bands, 1, out, slots)
+    groups = out.shape[0]
+    out = out.reshape(groups, -1, SUBLANES, LANES)
+    return jnp.swapaxes(out, 1, 2).reshape(groups * SUBLANES, -1)
 
 
 def solution(mesh):

time: 656 us -> 550 us (0.84); the launches traced: 656 us -> 542 us
  waiting for transfers between devices: 356 us -> 238 us
  Pallas kernels: 238 us -> 170 us
  local copies, waits for them, and re-layouts: 8.51 us -> 65.4 us
  other arithmetic: 33.4 us -> 42 us
    all_to_all x2 -> x5, waiting for transfers between devices: 356 us -> 238 us  [local(): swap = lambda value: lax.all_to_all(value, AXES, 0, 0, tiled=True)]
    pallas_call x2 -> x4, Pallas kernels: 197 us -> 125 us  [the longest x2 99.6 us: correlate_stage(): pl.pallas_call(functools.partial(correlate_kernel, devices, slots, pad, l...]
    slice x4 -> x16, local copies, waits for them, and re-layouts: 5.12 us -> 53.4 us  [the longest x3 27.4 us: edge_lines(): final = lambda a: a[:, 1, :, inside - 1::inside, count - 1]]
    all_to_all x2 -> x5, starting transfers between devices: 11 us -> 25 us  [local(): swap = lambda value: lax.all_to_all(value, AXES, 0, 0, tiled=True)]
    ppermute x2 -> x0, starting transfers between devices: 9.15 us -> none  [the longest x1 7.24 us: halo_lines(): following = lax.ppermute(head, AXES, backward)]
    unnamed x8 -> x1, other arithmetic: 7.66 us -> 0.01 us
    sin x4 -> x8, other arithmetic: 10.2 us -> 17.5 us  [phases(): return (jnp.cos(angles), jnp.sin(angles))]
    pallas_call x1 -> x2, Pallas kernels: 35.6 us -> 39.7 us  [row_stage(): pl.pallas_call(row_kernel, grid_spec=pltpu.PrefetchScalarGridSpec(num_sca...]
  transfers between devices with their start and end apart: 4 -> 5, of which waited for: 2 -> 4; matrix products, arithmetic and copies ran while one was open for 2% -> 13% of each run, Pallas kernels for 1% -> 19%
where the time goes in v2:
time: 550 us; the launch traced here: 542 us
  waiting for transfers between devices  238 us (43%)
  Pallas kernels  170 us (31%)
  local copies, waits for them, and re-layouts  65.4 us (12%)
  other arithmetic  42 us (8%)
  starting transfers between devices  25 us (5%)
    all_to_all x5, waiting for transfers between devices, local(): swap = lambda value: lax.all_to_all(value, AXES, 0, 0, tiled=True)  238 us
    pallas_call x2, Pallas kernels, correlate_stage(): pl.pallas_call(functools.partial(correlate_kernel, devices, slots, pad, l...  99.6 us
    pallas_call x2, Pallas kernels, row_stage(): pl.pallas_call(row_kernel, grid_spec=pltpu.PrefetchScalarGridSpec(num_sca...  39.7 us
    slice x3, local copies, waits for them, and re-layouts, edge_lines(): final = lambda a: a[:, 1, :, inside - 1::inside, count - 1]  27.4 us
    pallas_call x2, Pallas kernels, column_stage(): pl.pallas_call(functools.partial(column_kernel, part == 0), grid=(2 * chu...  25.5 us
    slice x3, local copies, waits for them, and re-layouts, edge_lines(): first = lambda a: a[:, 0, :, ::inside, 0]  25.3 us
    all_to_all x5, starting transfers between devices, local(): swap = lambda value: lax.all_to_all(value, AXES, 0, 0, tiled=True)  25 us
    sin x8, other arithmetic, phases(): return (jnp.cos(angles), jnp.sin(angles))  17.5 us
  transfers between devices with their start and end apart: 5, of which 4 were waited for; matrix products, arithmetic and copies ran while one was open for 13% of the time, Pallas kernels for 19%

profile of v2, /device:TPU:4, one launch (start us, length us, event | category | flops | bytes accessed | tf_op | source)
XLA Modules:
  0.0 542.2 jit_solution(7802489412279513794)
XLA Ops:
  0.2 0.7 broadcast_subtract_fusion
  0.9 0.8 fusion.76
  2.3 0.1 copy.84
  2.4 1.2 multiply_sine_fusion.2
  3.6 0.6 pad.28.clone
  4.2 1.7 fusion.68
  6.0 0.7 copy.93
  6.7 0.7 copy.92
  7.5 0.1 pad_maximum_fusion.7
  7.6 0.7 copy.86
  8.3 0.7 copy.90
  9.1 0.7 copy.87
  9.8 0.8 copy.91
  10.6 0.8 copy.89
  11.3 0.8 copy.88
  12.1 0.2 copy.85
  12.3 2.7 multiply_sine_fusion
  15.0 2.4 fusion.65
  17.4 4.2 fusion.40
  21.6 4.4 fusion.18
  26.0 0.7 maximum_bitcast_fusion
  26.7 1.9 maximum_multiply_fusion
  28.6 2.0 mul.846
  30.6 1.4 fusion.1
  32.0 5.3 bands.1.refs_3_.refs_2_
  37.5 0.2 fusion.5
  37.7 1.3 pad_maximum_fusion.3.first_ref
  39.0 1.8 pad_maximum_fusion.1.second_ref
  40.9 0.3 fusion.2
  41.2 1.6 pad_maximum_fusion.2.turn_ref
  42.8 12.7 %columns.3 = f32[256,4,8,128]{3,2,1,0:T(8,128)} custom-call(f32[2,1024,1024]{2,1,0:T(8,128)} %refs_3_.3, f32[2,1024,1024]{2,1,0:T(8,128)} %refs_3_.3, f32[2,1024,1024]{2,1,0:T(8,128)} %refs_3_.3, f32[2,1024,1024]{2,1,0:T(8,128)} %refs_3_.3, f32[256,128]{1,0:T(8,128)} %get-tuple-element.80.refs_4_, f32[256,128]{1,0:T(8,128)} %get-tuple-element.79.refs_5_, ...), custom_call_target="tpu_custom_call" | custom-call | flops 6442450944 | bytes 12582912 | tf_op jit(solution)/shard_map/columns/pallas_call | solution.py:329
  55.5 6.2 %all-to-all-start.1 = ((f32[32,8,4,8,128]{4,3,2,1,0:T(8,128)}), f32[32,8,4,8,128]{4,3,2,1,0:T(8,128)}, u32[]{:S(2)}, u32[]{:S(2)}) async-start(f32[32,8,4,8,128]{4,3,2,1,0:T(8,128)} %bitcast.77), calls=%async_computation.1 | async-start | bytes 8388608 | tf_op jit(solution)/shard_map/all_to_all | solution.py:713
  61.8 0.2 copy.83
  62.0 1.2 fusion.59
  63.3 1.2 multiply_sine_fusion.3
  64.4 2.7 multiply_sine_fusion.1
  67.1 12.8 %columns.2 = f32[256,4,8,128]{3,2,1,0:T(8,128)} custom-call(f32[2,1024,1024]{2,1,0:T(8,128)} %refs_3_.3, f32[2,1024,1024]{2,1,0:T(8,128)} %refs_3_.3, f32[2,1024,1024]{2,1,0:T(8,128)} %refs_3_.3, f32[2,1024,1024]{2,1,0:T(8,128)} %refs_3_.3, f32[256,128]{1,0:T(8,128)} %get-tuple-element.92.refs_4_, f32[256,128]{1,0:T(8,128)} %get-tuple-element.91.refs_5_, ...), custom_call_target="tpu_custom_call" | custom-call | flops 6442450944 | bytes 12582912 | tf_op jit(solution)/shard_map/columns/pallas_call | solution.py:329
  79.9 75.6 %all-to-all-done.1.x_ref = f32[32,8,4,8,128]{4,3,2,1,0:T(8,128)} async-done(((f32[32,8,4,8,128]{4,3,2,1,0:T(8,128)}), f32[32,8,4,8,128]{4,3,2,1,0:T(8,128)}, u32[]{:S(2)}, u32[]{:S(2)}) %all-to-all-start.1) | async-done | bytes 4194336 | tf_op jit(solution)/shard_map/all_to_all | solution.py:713
  155.6 4.6 all-to-all-start
  160.2 0.5 broadcast_31_variant_ref.2.variant_ref
  160.7 19.9 %rows.3 = (f32[32,2,8,8,128]{4,3,2,1,0:T(8,128)}, f32[32,2,8,8,128]{4,3,2,1,0:T(8,128)}) custom-call(s32[8]{0:T(128)} %broadcast_31_variant_ref.2.variant_ref, f32[32,8,4,8,128]{4,3,2,1,0:T(8,128)} %all-to-all-done.1.x_ref, bf16[2,512,768]{2,1,0:T(8,128)(2,1)} %pad_maximum_fusion.3.first_ref, f32[2,2,2,128,512]{4,3,2,1,0:T(8,128)} %pad_maximum_fusion.2.turn_ref, ...), custom_call_target="tpu_custom_call" | custom-call | flops 9663676416 | bytes 8388608 | tf_op jit(solution)/shard_map/rows/pallas_call | solution.py:434
  180.6 73.7 %all-to-all-done.x_ref = f32[32,8,4,8,128]{4,3,2,1,0:T(8,128)} async-done(((f32[32,8,4,8,128]{4,3,2,1,0:T(8,128)}), f32[32,8,4,8,128]{4,3,2,1,0:T(8,128)}, u32[]{:S(2)}, u32[]{:S(2)}) %all-to-all-start) | async-done | bytes 4194336 | tf_op jit(solution)/shard_map/all_to_all | solution.py:713
  254.3 3.8 all-to-all-start.4
  258.1 0.5 and_select_fusion.variant_ref
  258.6 19.9 %rows.2 = (f32[32,2,8,8,128]{4,3,2,1,0:T(8,128)}, f32[32,2,8,8,128]{4,3,2,1,0:T(8,128)}) custom-call(s32[8]{0:T(128)} %and_select_fusion.variant_ref, f32[32,8,4,8,128]{4,3,2,1,0:T(8,128)} %all-to-all-done.x_ref, bf16[2,512,768]{2,1,0:T(8,128)(2,1)} %pad_maximum_fusion.3.first_ref, f32[2,2,2,128,512]{4,3,2,1,0:T(8,128)} %pad_maximum_fusion.2.turn_ref, ...), custom_call_target="tpu_custom_call" | custom-call | flops 9663676416 | bytes 8388608 | tf_op jit(solution)/shard_map/rows/pallas_call | solution.py:434
  278.5 12.5 %slice.69 = f32[32,1,8,2,1]{4,3,2,1,0:T(2,128)S(1)} slice(f32[32,2,8,8,128]{4,3,2,1,0:T(8,128)} %get-tuple-element.17), slice={[0:32:1], [0:1:1], [0:8:1], [0:8:4], [0:1:1]} | slice | bytes 4096 | tf_op jit(solution)/shard_map/slice | solution.py:646
  291.1 13.6 %slice.66 = f32[32,1,8,2,1]{4,3,2,1,0:T(2,128)S(1)} slice(f32[32,2,8,8,128]{4,3,2,1,0:T(8,128)} %get-tuple-element.17), slice={[0:32:1], [1:2:1], [0:8:1], [3:8:4], [127:128:1]} | slice | bytes 4096 | tf_op jit(solution)/shard_map/slice | solution.py:647
  304.7 12.5 %slice.71 = f32[32,1,8,2,1]{4,3,2,1,0:T(2,128)S(1)} slice(f32[32,2,8,8,128]{4,3,2,1,0:T(8,128)} %get-tuple-element.20), slice={[0:32:1], [0:1:1], [0:8:1], [0:8:4], [0:1:1]} | slice | bytes 4096 | tf_op jit(solution)/shard_map/slice | solution.py:646
  317.2 13.6 %slice.70 = f32[32,1,8,2,1]{4,3,2,1,0:T(2,128)S(1)} slice(f32[32,2,8,8,128]{4,3,2,1,0:T(8,128)} %get-tuple-element.20), slice={[0:32:1], [1:2:1], [0:8:1], [3:8:4], [127:128:1]} | slice | bytes 4096 | tf_op jit(solution)/shard_map/slice | solution.py:647
  330.9 0.2 copy.97
  331.1 0.2 copy.96
  331.3 0.2 copy.99
  331.5 0.2 copy.98
  331.9 3.1 select_maximum_fusion
  335.1 1.4 copy-done.3
  336.4 5.9 %all-to-all-start.3 = ((f32[32,17,8,128]{3,2,1,0:T(8,128)}), f32[32,17,8,128]{3,2,1,0:T(8,128)S(1)}, u32[]{:S(2)}, u32[]{:S(2)}) async-start(f32[32,17,8,128]{3,2,1,0:T(8,128)} %select_maximum_fusion), calls=%async_computation.3 | async-start | bytes 4456448 | tf_op jit(solution)/shard_map/all_to_all | solution.py:713
  342.4 4.6 pad_maximum_fusion
  347.0 46.9 %all-to-all-done.3 = f32[32,17,8,128]{3,2,1,0:T(8,128)S(1)} async-done(((f32[32,17,8,128]{3,2,1,0:T(8,128)}), f32[32,17,8,128]{3,2,1,0:T(8,128)S(1)}, u32[]{:S(2)}, u32[]{:S(2)}) %all-to-all-start.3) | async-done | bytes 2228256 | tf_op jit(solution)/shard_map/all_to_all | solution.py:713
  394.0 4.4 all-to-all-start.2
  399.2 0.7 select_maximum_fusion.1.refs_2_
  399.9 0.7 select_maximum_fusion.2.refs_1_
  400.5 49.8 %correlate.2.refs_3_ = f32[2,65536,128]{2,1,0:T(8,128)} custom-call(f32[4352,128]{1,0:T(8,128)} %bitcast.79, f32[4096,128]{1,0:T(8,128)} %bitcast.80, f32[4,128]{1,0:T(4,128)} %select_maximum_fusion.1.refs_2_, bf16[8,768,256]{2,1,0:T(8,128)(2,1)} %bands.1.refs_3_.refs_2_), custom_call_target="tpu_custom_call" | custom-call | flops 1610612736 | bytes 33554432 | tf_op jit(solution)/shard_map/correlate/pallas_call | solution.py:616
  450.4 42.1 %all-to-all-done.2 = f32[32,32,8,128]{3,2,1,0:T(8,128)} async-done(((f32[32,32,8,128]{3,2,1,0:T(8,128)}), f32[32,32,8,128]{3,2,1,0:T(8,128)}, u32[]{:S(2)}, u32[]{:S(2)}) %all-to-all-start.2) | async-done | bytes 4194336 | tf_op jit(solution)/shard_map/all_to_all | solution.py:713
  492.5 49.8 %correlate.3 = f32[2,65536,128]{2,1,0:T(8,128)} custom-call(f32[8192,128]{1,0:T(8,128)} %bitcast.26.refs_0_, f32[4,128]{1,0:T(4,128)} %select_maximum_fusion.2.refs_1_, bf16[8,768,256]{2,1,0:T(8,128)(2,1)} %bands.1.refs_3_.refs_2_, f32[2,65536,128]{2,1,0:T(8,128)} %correlate.2.refs_3_), custom_call_target="tpu_custom_call", output_to_operand_aliasing={{}: (3, {})} | custom-call | flops 1610612736 | bytes 33554432 | tf_op jit(solution)/shard_map/correlate/pallas_call | solution.py:616
  (85 shorter events, 2.1 us)
Async XLA Ops:
  0.0 0.9 copy-start
  32.0 5.4 copy-start.10
  32.0 5.4 copy-start.11
  32.0 5.4 copy-start.14
  32.0 5.4 copy-start.16
  32.0 5.4 %copy-start.12 = (f32[128,256]{1,0:T(8,128)S(1)}, f32[128,256]{1,0:T(8,128)}, u32[]{:S(2)}) copy-start(f32[128,256]{1,0:T(8,128)} %copy.86) | copy-start | bytes 393220
  32.0 5.4 %copy-start.13 = (f32[128,256]{1,0:T(8,128)S(1)}, f32[128,256]{1,0:T(8,128)}, u32[]{:S(2)}) copy-start(f32[128,256]{1,0:T(8,128)} %copy.87) | copy-start | bytes 393220
  32.0 5.4 %copy-start.15 = (f32[128,256]{1,0:T(8,128)S(1)}, f32[128,256]{1,0:T(8,128)}, u32[]{:S(2)}) copy-start(f32[128,256]{1,0:T(8,128)} %copy.89) | copy-start | bytes 393220
  32.0 5.4 %copy-start.17 = (f32[128,256]{1,0:T(8,128)S(1)}, f32[128,256]{1,0:T(8,128)}, u32[]{:S(2)}) copy-start(f32[128,256]{1,0:T(8,128)} %copy.88) | copy-start | bytes 393220
  37.5 1.5 copy-start.4
  38.9 1.8 copy-start.5
  38.9 1.9 copy-start.6
  38.9 1.9 copy-start.7
  39.0 1.9 copy-start.8
  39.0 1.9 copy-start.9
  55.5 100.1 %all-to-all-start.1 = ((f32[32,8,4,8,128]{4,3,2,1,0:T(8,128)}), f32[32,8,4,8,128]{4,3,2,1,0:T(8,128)}, u32[]{:S(2)}, u32[]{:S(2)}) async-start(f32[32,8,4,8,128]{4,3,2,1,0:T(8,128)} %bitcast.77), calls=%async_computation.1 | async-start | bytes 8388608 | tf_op jit(solution)/shard_map/all_to_all | solution.py:713
  155.6 98.7 %all-to-all-start = ((f32[32,8,4,8,128]{4,3,2,1,0:T(8,128)}), f32[32,8,4,8,128]{4,3,2,1,0:T(8,128)}, u32[]{:S(2)}, u32[]{:S(2)}) async-start(f32[32,8,4,8,128]{4,3,2,1,0:T(8,128)} %bitcast.78), calls=%async_computation | async-start | bytes 8388608 | tf_op jit(solution)/shard_map/all_to_all | solution.py:713
  254.3 80.8 %all-to-all-start.4 = ((f32[32,16,8,128]{3,2,1,0:T(8,128)}), f32[32,16,8,128]{3,2,1,0:T(8,128)S(1)}, u32[]{:S(2)}, u32[]{:S(2)}) async-start(f32[32,16,8,128]{3,2,1,0:T(8,128)} %bitcast.83), calls=%async_computation.4 | async-start | bytes 4194304 | tf_op jit(solution)/shard_map/all_to_all | solution.py:713
  335.1 1.4 copy-start.3
  336.4 57.5 %all-to-all-start.3 = ((f32[32,17,8,128]{3,2,1,0:T(8,128)}), f32[32,17,8,128]{3,2,1,0:T(8,128)S(1)}, u32[]{:S(2)}, u32[]{:S(2)}) async-start(f32[32,17,8,128]{3,2,1,0:T(8,128)} %select_maximum_fusion), calls=%async_computation.3 | async-start | bytes 4456448 | tf_op jit(solution)/shard_map/all_to_all | solution.py:713
  394.0 4.5 copy-start.2
  394.0 98.5 %all-to-all-start.2 = ((f32[32,32,8,128]{3,2,1,0:T(8,128)}), f32[32,32,8,128]{3,2,1,0:T(8,128)}, u32[]{:S(2)}, u32[]{:S(2)}) async-start(f32[32,32,8,128]{3,2,1,0:T(8,128)} %pad_maximum_fusion), calls=%async_computation.2 | async-start | bytes 8388608 | tf_op jit(solution)/shard_map/all_to_all | solution.py:713
  492.5 49.8 %copy-start.1 = (f32[200,128]{1,0:T(8,128)S(1)}, f32[200,128]{1,0:T(8,128)}, u32[]{:S(2)}) copy-start(f32[200,128]{1,0:T(8,128)} %param.5) | copy-start | bytes 307204

commit v3 on v2

--- a/solution.py
+++ b/solution.py
@@ -14,6 +14,7 @@
 SUBLANES = 8
 VMEM_LIMIT = 60 * 1024 * 1024
 PARTS = 2
+SHARES = (1, 3)
 F32 = jnp.float32
 BF16 = jnp.bfloat16
 
@@ -302,13 +303,12 @@
         o_ref[slot, 0] = stage[pl.ds(slot, SUBLANES, stride=span), :]
 
 
-def column_stage(series, position, width, part):
+def column_stage(series, position, width, first_slot, slots):
     rows, cols = series.shape[1], series.shape[2]
-    slots = rows // 2 // PARTS
     inner = cols // width
     chunks = width // LANES
     samples = 2 * rows * cols * lax.axis_size(AXES)
-    slot = part * slots + iota(slots)
+    slot = first_slot + iota(slots)
     near_re, near_im = phases(slot[:, None] * iota(LANES)[None, :], rows)
     far_re, far_im = phases(slot[:, None] * (LANES * iota(rows // LANES))[None, :], rows)
     base_re, base_im = phases(slot[:, None] * (2 * iota(LANES))[None, :], samples)
@@ -327,7 +327,7 @@
     )
     tables = (near_re, near_im, far_re, far_im, base_re, base_im)
     return pl.pallas_call(
-        functools.partial(column_kernel, part == 0),
+        functools.partial(column_kernel, first_slot == 0),
         grid=(2 * chunks,),
         in_specs=[column(block) for block in range(inner)]
         + [whole(table) for table in tables]
@@ -489,14 +489,14 @@
 
 
 def correlate_kernel(
-    devices, slots, pad, inputs, *refs
+    devices, counts, pad, inputs, *refs
 ):
     x_refs, (halo_ref, band_ref) = refs[:inputs], refs[inputs : inputs + 2]
     o_ref, table, last, lhs, stage_a, stage_b = refs[-6:]
     step = pl.program_id(0)
     steps = pl.num_programs(0)
     inside = SUBLANES // 2
-    total = 2 * PARTS * devices * slots
+    total = 2 * devices * sum(counts)
     pitch = total + pad
     half = LANES // 2
     taps_half = half // 2
@@ -506,13 +506,14 @@
         def source(s, carry):
             for part in range(PARTS):
                 for side in range(2):
-                    for slot in range(slots):
+                    for slot in range(counts[part]):
                         x_ref = x_refs[min(part, inputs - 1)]
                         tiles = x_ref.shape[0] // devices // SUBLANES
-                        place = (part * 2 + side if inputs < PARTS else side) * slots + slot
+                        place = side * counts[part] + slot
+                        place += 2 * sum(counts[:part]) if inputs < PARTS else 0
                         start = (s * tiles + place) * SUBLANES
                         tile = x_ref[pl.ds(pl.multiple_of(start, SUBLANES), SUBLANES), :]
-                        row = (part * devices + s) * slots + slot
+                        row = devices * sum(counts[:part]) + s * counts[part] + slot
                         if side == 1:
                             row = total - row
                             if slot == 0 and part == 0:
@@ -600,9 +601,9 @@
     emit(chunks - 1, groups - 1, stages[(groups - 1) % 2])
 
 
-def correlate_stage(arrived, halo, bands, part, earlier, slots):
+def correlate_stage(arrived, halo, bands, part, earlier, counts):
     devices, _, _, count = arrived[0].shape
-    total = 2 * PARTS * devices * slots
+    total = 2 * devices * sum(counts)
     drifts = 2 * bands.shape[0]
     groups = drifts // SUBLANES
     pad = SUBLANES
@@ -614,7 +615,7 @@
     )
     extra = [] if earlier is None else [earlier]
     return pl.pallas_call(
-        functools.partial(correlate_kernel, devices, slots, pad, len(flat)),
+        functools.partial(correlate_kernel, devices, counts, pad, len(flat)),
         grid=(inside,),
         in_specs=[resident(a.shape) for a in flat]
         + [resident(halo.shape), resident(bands.shape)]
@@ -692,7 +693,7 @@
     return (
         2 * LANES // devices == SUBLANES
         and lines // devices == SUBLANES
-        and rows % (2 * devices * SUBLANES) == 0
+        and rows % (2 * devices * sum(SHARES)) == 0
         and drifts % SUBLANES == 0
         and 2 * taps == LANES
     )
@@ -706,7 +707,7 @@
     if not fits(series.shape, devices, drift_template.shape[0], taps):
         return general_local(series, templates, drift_template, drift_reach)
     width = devices * cols // LANES
-    slots = rows // 2 // devices // PARTS
+    counts = tuple(rows // 2 // devices * share // sum(SHARES) for share in SHARES)
     samples = 2 * rows * cols * devices
     chunks = 2 * width // LANES
     arrived = []
@@ -714,24 +715,26 @@
     tables = row_tables(devices, chunks, SUBLANES, samples)
     bands = band_stage(*tap_kernels(templates, drift_template, drift_reach))
     for part in range(PARTS):
-        columns = column_stage(series, position, width, part)
-        columns = columns.reshape(devices, slots, chunks, SUBLANES, LANES)
+        columns = column_stage(
+            series, position, width, devices * sum(counts[:part]), devices * counts[part]
+        )
+        columns = columns.reshape(devices, counts[part], chunks, SUBLANES, LANES)
         if part == PARTS - 1:
-            columns, tables, bands = lax.optimization_barrier((columns, tables, bands))
+            columns, bands = lax.optimization_barrier((columns, bands))
         arrived.append(swap(columns))
     pieces = []
     for part in range(PARTS):
         spectra = row_stage(arrived[part], tables, position, part)
-        tiles = [a.reshape(devices, 2 * slots, SUBLANES, LANES) for a in spectra]
+        tiles = [a.reshape(devices, 2 * counts[part], SUBLANES, LANES) for a in spectra]
         if part == 0:
             tiles[0] = jnp.concatenate([tiles[0], edge_lines(spectra)], axis=1)
         pieces.append(tiles)
     first = swap(pieces[0][0])
     second = swap(pieces[1][0])
     rest = swap(jnp.concatenate([pieces[0][1], pieces[1][1]], axis=1))
-    halos = halo_lines(first[:, 2 * slots], slots, taps)
-    out = correlate_stage([first, second], halos[0], bands, 0, None, slots)
-    out = correlate_stage([rest], halos[1], bands, 1, out, slots)
+    halos = halo_lines(first[:, 2 * counts[0]], counts[0], taps)
+    out = correlate_stage([first, second], halos[0], bands, 0, None, counts)
+    out = correlate_stage([rest], halos[1], bands, 1, out, counts)
     groups = out.shape[0]
     out = out.reshape(groups, -1, SUBLANES, LANES)
     return jnp.swapaxes(out, 1, 2).reshape(groups * SUBLANES, -1)

time: 550 us -> 481 us (0.87)
  waiting for transfers between devices: 238 us -> 180 us
    all_to_all x5, waiting for transfers between devices: 238 us -> 180 us  [local(): swap = lambda value: lax.all_to_all(value, AXES, 0, 0, tiled=True)]
    sin x8 -> x9, other arithmetic: 17.5 us -> 18.2 us  [phases(): return (jnp.cos(angles), jnp.sin(angles))]
  transfers between devices with their start and end apart: 5 -> 5, of which waited for: 4 -> 5; matrix products, arithmetic and copies ran while one was open for 13% -> 19% of each run, Pallas kernels for 19% -> 24%
where the time goes in v3:
time: 481 us; the launch traced here: 474 us
  waiting for transfers between devices  180 us (37%)
  Pallas kernels  171 us (36%)
  local copies, waits for them, and re-layouts  60.5 us (13%)
  other arithmetic  38.3 us (8%)
  starting transfers between devices  23.8 us (5%)
    all_to_all x5, waiting for transfers between devices, local(): swap = lambda value: lax.all_to_all(value, AXES, 0, 0, tiled=True)  180 us
    pallas_call x2, Pallas kernels, correlate_stage(): pl.pallas_call(functools.partial(correlate_kernel, devices, counts, pad,...  99.6 us
    pallas_call x2, Pallas kernels, row_stage(): pl.pallas_call(row_kernel, grid_spec=pltpu.PrefetchScalarGridSpec(num_sca...  39.6 us
    pallas_call x2, Pallas kernels, column_stage(): pl.pallas_call(functools.partial(column_kernel, first_slot == 0), grid=(2...  26.4 us
    slice x3, local copies, waits for them, and re-layouts, edge_lines(): final = lambda a: a[:, 1, :, inside - 1::inside, count - 1]  25.9 us
    all_to_all x5, starting transfers between devices, local(): swap = lambda value: lax.all_to_all(value, AXES, 0, 0, tiled=True)  23.8 us
    slice x3, local copies, waits for them, and re-layouts, edge_lines(): first = lambda a: a[:, 0, :, ::inside, 0]  23.7 us
    sin x9, other arithmetic, phases(): return (jnp.cos(angles), jnp.sin(angles))  18.2 us
  transfers between devices with their start and end apart: 5, of which 5 were waited for; matrix products, arithmetic and copies ran while one was open for 19% of the time, Pallas kernels for 24%

profile of v3, /device:TPU:4, one launch (start us, length us, event | category | flops | bytes accessed | tf_op | source)
XLA Modules:
  0.0 474.2 jit_solution(11163793280993501878)
XLA Ops:
  0.0 0.9 fusion.68
  1.3 0.9 multiply_sine_fusion.3
  2.2 0.9 fusion.70
  3.1 0.1 copy.84
  3.3 1.7 multiply_sine_fusion.1
  5.0 8.7 %columns.2 = f32[128,4,8,128]{3,2,1,0:T(8,128)} custom-call(f32[2,1024,1024]{2,1,0:T(8,128)} %refs_3_.3, f32[2,1024,1024]{2,1,0:T(8,128)} %refs_3_.3, f32[2,1024,1024]{2,1,0:T(8,128)} %refs_3_.3, f32[2,1024,1024]{2,1,0:T(8,128)} %refs_3_.3, f32[128,128]{1,0:T(8,128)} %get-tuple-element.82.refs_4_, f32[128,128]{1,0:T(8,128)} %get-tuple-element.81.refs_5_, ...), custom_call_target="tpu_custom_call" | custom-call | flops 3221225472 | bytes 12582912 | tf_op jit(solution)/shard_map/columns/pallas_call | solution.py:329
  13.7 6.1 %all-to-all-start = ((f32[32,4,4,8,128]{4,3,2,1,0:T(8,128)}), f32[32,4,4,8,128]{4,3,2,1,0:T(8,128)S(1)}, u32[]{:S(2)}, u32[]{:S(2)}) async-start(f32[32,4,4,8,128]{4,3,2,1,0:T(8,128)} %bitcast.81), calls=%async_computation | async-start | bytes 4194304 | tf_op jit(solution)/shard_map/all_to_all | solution.py:714
  19.8 0.2 fusion.74
  20.0 0.1 fusion.81
  20.2 0.1 copy.94
  20.5 0.3 copy.95
  20.8 0.6 pad.28.clone
  21.4 5.3 %bands.1.refs_3_.refs_2_ = bf16[8,768,256]{2,1,0:T(8,128)(2,1)} custom-call(f32[8,4,128]{2,1,0:T(4,128)} %bitcast.97), custom_call_target="tpu_custom_call" | custom-call | tf_op jit(solution)/shard_map/bands/pallas_call | solution.py:481
  26.7 1.5 multiply_sine_fusion.2
  28.1 2.5 fusion.40
  30.7 3.6 multiply_sine_fusion
  34.3 17.7 %columns.3 = f32[384,4,8,128]{3,2,1,0:T(8,128)} custom-call(f32[2,1024,1024]{2,1,0:T(8,128)} %refs_3_.3, f32[2,1024,1024]{2,1,0:T(8,128)} %refs_3_.3, f32[2,1024,1024]{2,1,0:T(8,128)} %refs_3_.3, f32[2,1024,1024]{2,1,0:T(8,128)} %refs_3_.3, f32[384,128]{1,0:T(8,128)} %get-tuple-element.72.refs_4_, f32[384,128]{1,0:T(8,128)} %get-tuple-element.71.refs_5_, ...), custom_call_target="tpu_custom_call" | custom-call | flops 9663676416 | bytes 12582912 | tf_op jit(solution)/shard_map/columns/pallas_call | solution.py:329
  52.0 16.6 %all-to-all-done.x_ref = f32[32,4,4,8,128]{4,3,2,1,0:T(8,128)S(1)} async-done(((f32[32,4,4,8,128]{4,3,2,1,0:T(8,128)}), f32[32,4,4,8,128]{4,3,2,1,0:T(8,128)S(1)}, u32[]{:S(2)}, u32[]{:S(2)}) %all-to-all-start) | async-done | bytes 2097184 | tf_op jit(solution)/shard_map/all_to_all | solution.py:714
  68.6 1.3 copy-done.4
  69.9 4.3 all-to-all-start.1
  74.4 1.7 fusion.64
  76.4 0.1 pad_maximum_fusion.7
  77.3 4.5 fusion.18
  81.7 0.7 maximum_bitcast_fusion
  82.4 2.0 maximum_multiply_fusion
  84.4 2.0 mul.864
  86.3 0.6 and_select_fusion.variant_ref
  86.9 3.1 fusion.37
  90.2 0.2 fusion.5
  90.5 1.3 pad_maximum_fusion.3.first_ref
  91.7 0.3 fusion.2
  92.0 1.6 pad_maximum_fusion.2.turn_ref
  93.6 0.4 fusion.1
  94.1 1.8 pad_maximum_fusion.1.second_ref
  95.9 11.9 %rows.2 = (f32[32,2,4,8,128]{4,3,2,1,0:T(8,128)}, f32[32,2,4,8,128]{4,3,2,1,0:T(8,128)}) custom-call(s32[4]{0:T(128)} %and_select_fusion.variant_ref, f32[32,4,4,8,128]{4,3,2,1,0:T(8,128)} %copy-done.4, bf16[2,512,768]{2,1,0:T(8,128)(2,1)} %pad_maximum_fusion.3.first_ref, f32[2,2,2,128,512]{4,3,2,1,0:T(8,128)} %pad_maximum_fusion.2.turn_ref, ...), custom_call_target="tpu_custom_call" | custom-call | flops 4831838208 | bytes 4194304 | tf_op jit(solution)/shard_map/rows/pallas_call | solution.py:434
  107.8 11.8 %slice.69 = f32[32,1,4,2,1]{4,3,2,1,0:T(2,128)S(1)} slice(f32[32,2,4,8,128]{4,3,2,1,0:T(8,128)} %get-tuple-element.11), slice={[0:32:1], [0:1:1], [0:4:1], [0:8:4], [0:1:1]} | slice | bytes 2048 | tf_op jit(solution)/shard_map/slice | solution.py:647
  119.7 12.9 %slice.66 = f32[32,1,4,2,1]{4,3,2,1,0:T(2,128)S(1)} slice(f32[32,2,4,8,128]{4,3,2,1,0:T(8,128)} %get-tuple-element.11), slice={[0:32:1], [1:2:1], [0:4:1], [3:8:4], [127:128:1]} | slice | bytes 2048 | tf_op jit(solution)/shard_map/slice | solution.py:648
  132.6 11.7 %slice.71 = f32[32,1,4,2,1]{4,3,2,1,0:T(2,128)S(1)} slice(f32[32,2,4,8,128]{4,3,2,1,0:T(8,128)} %get-tuple-element.14), slice={[0:32:1], [0:1:1], [0:4:1], [0:8:4], [0:1:1]} | slice | bytes 2048 | tf_op jit(solution)/shard_map/slice | solution.py:647
  144.3 12.9 %slice.70 = f32[32,1,4,2,1]{4,3,2,1,0:T(2,128)S(1)} slice(f32[32,2,4,8,128]{4,3,2,1,0:T(8,128)} %get-tuple-element.14), slice={[0:32:1], [1:2:1], [0:4:1], [3:8:4], [127:128:1]} | slice | bytes 2048 | tf_op jit(solution)/shard_map/slice | solution.py:648
  157.2 0.1 copy.98
  157.4 0.1 copy.97
  157.5 0.1 copy.100
  157.6 0.1 copy.99
  157.9 0.1 copy.105
  158.0 1.1 select_maximum_fusion
  159.2 54.6 %all-to-all-done.1.x_ref = f32[32,12,4,8,128]{4,3,2,1,0:T(8,128)} async-done(((f32[32,12,4,8,128]{4,3,2,1,0:T(8,128)}), f32[32,12,4,8,128]{4,3,2,1,0:T(8,128)}, u32[]{:S(2)}, u32[]{:S(2)}) %all-to-all-start.1) | async-done | bytes 6291488 | tf_op jit(solution)/shard_map/all_to_all | solution.py:714
  213.7 3.8 all-to-all-start.3
  217.5 0.6 broadcast_33_variant_ref.2.variant_ref
  218.1 27.7 %rows.3 = (f32[32,2,12,8,128]{4,3,2,1,0:T(8,128)}, f32[32,2,12,8,128]{4,3,2,1,0:T(8,128)}) custom-call(s32[12]{0:T(128)} %broadcast_33_variant_ref.2.variant_ref, f32[32,12,4,8,128]{4,3,2,1,0:T(8,128)} %all-to-all-done.1.x_ref, bf16[2,512,768]{2,1,0:T(8,128)(2,1)} %pad_maximum_fusion.3.first_ref, f32[2,2,2,128,512]{4,3,2,1,0:T(8,128)} %pad_maximum_fusion.2.turn_ref, ...), custom_call_target="tpu_custom_call" | custom-call | flops 14495514624 | bytes 12582912 | tf_op jit(solution)/shard_map/rows/pallas_call | solution.py:434
  245.8 0.9 all-to-all-done.3
  246.7 1.0 copy-done.3
  247.7 5.0 %all-to-all-start.4 = ((f32[32,24,8,128]{3,2,1,0:T(8,128)}), f32[32,24,8,128]{3,2,1,0:T(8,128)S(1)}, u32[]{:S(2)}, u32[]{:S(2)}) async-start(f32[32,24,8,128]{3,2,1,0:T(8,128)} %bitcast.83), calls=%async_computation.4 | async-start | bytes 6291456 | tf_op jit(solution)/shard_map/all_to_all | solution.py:714
  252.8 4.6 pad_maximum_fusion
  257.4 66.7 %all-to-all-done.4 = f32[32,24,8,128]{3,2,1,0:T(8,128)S(1)} async-done(((f32[32,24,8,128]{3,2,1,0:T(8,128)}), f32[32,24,8,128]{3,2,1,0:T(8,128)S(1)}, u32[]{:S(2)}, u32[]{:S(2)}) %all-to-all-start.4) | async-done | bytes 3145760 | tf_op jit(solution)/shard_map/all_to_all | solution.py:714
  324.1 1.7 copy-done.2
  325.8 4.5 all-to-all-start.2
  330.3 0.9 slice_bitcast_fusion
  331.6 0.1 squeeze.21
  331.8 0.1 squeeze.18
  332.1 0.6 select_maximum_fusion.1.refs_2_
  332.7 0.7 select_maximum_fusion.2.refs_1_
  333.4 49.8 %correlate.2.refs_3_ = f32[2,65536,128]{2,1,0:T(8,128)} custom-call(f32[2304,128]{1,0:T(8,128)} %bitcast.82, f32[6144,128]{1,0:T(8,128)} %bitcast.80, f32[4,128]{1,0:T(4,128)} %select_maximum_fusion.1.refs_2_, bf16[8,768,256]{2,1,0:T(8,128)(2,1)} %bands.1.refs_3_.refs_2_), custom_call_target="tpu_custom_call" | custom-call | flops 1610612736 | bytes 33554432 | tf_op jit(solution)/shard_map/correlate/pallas_call | solution.py:617
  383.2 41.2 %all-to-all-done.2 = f32[32,32,8,128]{3,2,1,0:T(8,128)} async-done(((f32[32,32,8,128]{3,2,1,0:T(8,128)}), f32[32,32,8,128]{3,2,1,0:T(8,128)}, u32[]{:S(2)}, u32[]{:S(2)}) %all-to-all-start.2) | async-done | bytes 4194336 | tf_op jit(solution)/shard_map/all_to_all | solution.py:714
  424.4 49.8 %correlate.3 = f32[2,65536,128]{2,1,0:T(8,128)} custom-call(f32[8192,128]{1,0:T(8,128)} %bitcast.26.refs_0_, f32[4,128]{1,0:T(4,128)} %select_maximum_fusion.2.refs_1_, bf16[8,768,256]{2,1,0:T(8,128)(2,1)} %bands.1.refs_3_.refs_2_, f32[2,65536,128]{2,1,0:T(8,128)} %correlate.2.refs_3_), custom_call_target="tpu_custom_call", output_to_operand_aliasing={{}: (3, {})} | custom-call | flops 1610612736 | bytes 33554432 | tf_op jit(solution)/shard_map/correlate/pallas_call | solution.py:617
  (67 shorter events, 2.5 us)
Async XLA Ops:
  0.0 19.8 %copy-start = (f32[200,128]{1,0:T(8,128)S(1)}, f32[200,128]{1,0:T(8,128)}, u32[]{:S(2)}) copy-start(f32[200,128]{1,0:T(8,128)} %param.5) | copy-start | bytes 307204
  13.7 6.1 %copy-start.7 = (s32[16]{0:T(128)S(1)}, s32[16]{0:T(128)}, u32[]{:S(2)}) copy-start(s32[16]{0:T(128)} %param.7) | copy-start | bytes 196
  13.7 6.2 %copy-start.6 = (s32[16]{0:T(128)S(1)}, s32[16]{0:T(128)}, u32[]{:S(2)}) copy-start(s32[16]{0:T(128)} %param.6) | copy-start | bytes 196
  13.7 54.9 %all-to-all-start = ((f32[32,4,4,8,128]{4,3,2,1,0:T(8,128)}), f32[32,4,4,8,128]{4,3,2,1,0:T(8,128)S(1)}, u32[]{:S(2)}, u32[]{:S(2)}) async-start(f32[32,4,4,8,128]{4,3,2,1,0:T(8,128)} %bitcast.81), calls=%async_computation | async-start | bytes 4194304 | tf_op jit(solution)/shard_map/all_to_all | solution.py:714
  68.6 1.3 copy-start.4
  69.9 143.9 %all-to-all-start.1 = ((f32[32,12,4,8,128]{4,3,2,1,0:T(8,128)}), f32[32,12,4,8,128]{4,3,2,1,0:T(8,128)}, u32[]{:S(2)}, u32[]{:S(2)}) async-start(f32[32,12,4,8,128]{4,3,2,1,0:T(8,128)} %bitcast.79), calls=%async_computation.1 | async-start | bytes 12582912 | tf_op jit(solution)/shard_map/all_to_all | solution.py:714
  107.8 50.2 %copy-start.5 = (f32[32,2,4,8,128]{4,3,2,1,0:T(8,128)S(1)}, f32[32,2,4,8,128]{4,3,2,1,0:T(8,128)}, u32[]{:S(2)}) copy-start(f32[32,2,4,8,128]{4,3,2,1,0:T(8,128)} %get-tuple-element.14) | copy-start | bytes 3145732
  213.7 33.0 %all-to-all-start.3 = ((f32[32,9,8,128]{3,2,1,0:T(8,128)}), f32[32,9,8,128]{3,2,1,0:T(8,128)S(1)}, u32[]{:S(2)}, u32[]{:S(2)}) async-start(f32[32,9,8,128]{3,2,1,0:T(8,128)} %select_maximum_fusion), calls=%async_computation.3 | async-start | bytes 2359296 | tf_op jit(solution)/shard_map/all_to_all | solution.py:714
  246.7 1.0 copy-start.3
  247.7 76.3 %all-to-all-start.4 = ((f32[32,24,8,128]{3,2,1,0:T(8,128)}), f32[32,24,8,128]{3,2,1,0:T(8,128)S(1)}, u32[]{:S(2)}, u32[]{:S(2)}) async-start(f32[32,24,8,128]{3,2,1,0:T(8,128)} %bitcast.83), calls=%async_computation.4 | async-start | bytes 6291456 | tf_op jit(solution)/shard_map/all_to_all | solution.py:714
  324.1 1.7 copy-start.2
  325.8 98.6 %all-to-all-start.2 = ((f32[32,32,8,128]{3,2,1,0:T(8,128)}), f32[32,32,8,128]{3,2,1,0:T(8,128)}, u32[]{:S(2)}, u32[]{:S(2)}) async-start(f32[32,32,8,128]{3,2,1,0:T(8,128)} %pad_maximum_fusion), calls=%async_computation.2 | async-start | bytes 8388608 | tf_op jit(solution)/shard_map/all_to_all | solution.py:714
  424.4 49.8 %copy-start.1 = (f32[200,128]{1,0:T(8,128)S(1)}, f32[200,128]{1,0:T(8,128)}, u32[]{:S(2)}) copy-start(f32[200,128]{1,0:T(8,128)} %param.5) | copy-start | bytes 307204
